TPU v7x, 512 devices: a whole 4x4x16 slice. The times are simulated.
512 devices in a mesh: ctx: 32 (over z, core), dp: 16 (over x, y).
Axes of the slice: x: 4, y: 4, z: 16, core: 2. Of those that a mesh axis runs over, the one named last changes fastest.
Arguments:
- q_nope: bfloat16 [4096, 16384], P('ctx', 'dp'), may hold values from -6 to 6
- q_rope: bfloat16 [4096, 8192], P('ctx', 'dp'), may hold values from -400 to 400
- latent: bfloat16 [4096, 512], P('ctx'), may hold values from -6 to 6
- k_rope: bfloat16 [4096, 64], P('ctx'), may hold values from -5.2 to 5.2
- w_uk: bfloat16 [512, 16384], P('ctx', 'dp'), may hold values from -0.25 to 0.25
- w_uv: bfloat16 [512, 16384], P('ctx', 'dp'), may hold values from -0.25 to 0.25
- out_grad: bfloat16 [4096, 16384], P('ctx', 'dp'), may hold values from -6 to 6
- log_prob: float32 [4096], P('ctx'), may hold values from -5.4 to 0
- ref_logp: float32 [1], replicated, may hold values from -2.5 to -0.5
- doc_ids: int32 [4096], P('ctx'), may hold values from 0 to 31, never falling along the last dimension, each value on 1 to 256 neighbouring positions
- loss_mask: int32 [4096], P('ctx'), may hold values from 0 to 1, as said below
Outputs:
- dq_nope: bfloat16 [4096, 16384], P('ctx', 'dp')
- dq_rope: bfloat16 [4096, 8192], P('ctx', 'dp')
- d_latent: bfloat16 [4096, 512], P('ctx')
- d_krope: bfloat16 [4096, 64], P('ctx')
- dw_uk: float32 [512, 16384], P('ctx', 'dp')
- dw_uv: float32 [512, 16384], P('ctx', 'dp')
Inputs may be any that keep to these rules, and one draw needn't show every extreme that they name: `doc_ids`: each document is a run of consecutive positions of at most 256 tokens; numbers never fall along the sequence. `loss_mask`: the last token of the sequence counts.
All inputs are finite; a program needn't handle non-finite values.
Results may differ from a plain program's by a relative error of at most 0.03.
Values may be sent and summed in bfloat16 or wider, within the bound.
A program may use at most 64 MiB of HBM per device.

v0:
```python
import math

import jax
import jax.numpy as jnp
from jax import lax
from jax.sharding import PartitionSpec as P

NOPE = 128
ROPE = 64
VDIM = 128


npo_beta = 1.0


def shifted(block, axis, distance):
    devices = range(lax.axis_size(axis))
    route = [(i - distance, i) for i in devices if i - distance in devices]
    return lax.ppermute(block, axis, route)


def attend_head(query_nope, query_rope, key_nope, key_rope, values, grad_out, allowed):
    single = jnp.float32
    score_scale = 1.0 / math.sqrt(NOPE + ROPE)
    scores = jnp.einsum("qd,kd->qk", query_nope, key_nope, preferred_element_type=single)
    scores = scores + jnp.einsum("qd,kd->qk", query_rope, key_rope, preferred_element_type=single)
    scores = jnp.where(allowed, scores * score_scale, -1e30)
    row_max = jnp.max(scores, axis=1, keepdims=True)
    expon = jnp.where(allowed, jnp.exp(scores - row_max), 0.0)
    probs = expon / jnp.sum(expon, axis=1, keepdims=True)
    probs_low = probs.astype(jnp.bfloat16)
    attn_out = jnp.einsum("qk,kd->qd", probs_low, values, preferred_element_type=single)
    delta = jnp.sum(attn_out * grad_out.astype(single), axis=1)
    dprob = jnp.einsum("qd,kd->qk", grad_out, values, preferred_element_type=single)
    dscore = (probs * (dprob - delta[:, None]) * score_scale).astype(jnp.bfloat16)
    dq_nope = jnp.einsum("qk,kd->qd", dscore, key_nope, preferred_element_type=single).astype(
        jnp.bfloat16
    )
    dq_rope = jnp.einsum("qk,kd->qd", dscore, key_rope, preferred_element_type=single).astype(
        jnp.bfloat16
    )
    part_nope = jnp.einsum("qk,qd->kd", dscore, query_nope, preferred_element_type=single).astype(
        jnp.bfloat16
    )
    part_rope = jnp.einsum("qk,qd->kd", dscore, query_rope, preferred_element_type=single)
    part_value = jnp.einsum("qk,qd->kd", probs_low, grad_out, preferred_element_type=single).astype(
        jnp.bfloat16
    )
    return (dq_nope, dq_rope, part_nope, part_value, part_rope)


def head_major(array, rows, count, width):
    return array.reshape(rows, count, width).transpose(1, 0, 2)


def row_major(array, rows, count, width):
    return array.transpose(1, 0, 2).reshape(rows, count * width)


def on_device(
    q_nope, q_rope, latent, k_rope, w_uk, w_uv, out_grad, log_prob, ref_logp, doc_ids, loss_mask
):
    block_rows = latent.shape[0]
    width_nope = w_uk.shape[1]
    head_count = width_nope // NOPE
    highest = lax.Precision.HIGHEST
    position = lax.axis_index("ctx")
    full_uk, full_uv = (
        lax.all_gather(w_uk, "ctx", axis=0, tiled=True),
        lax.all_gather(w_uv, "ctx", axis=0, tiled=True),
    )
    mask_f = loss_mask.astype(jnp.float32)
    live_total, live_count = lax.psum((jnp.sum(mask_f * log_prob), jnp.sum(mask_f)), "ctx")
    seq_len = block_rows * lax.axis_size("ctx")
    npo_weight = (
        2.0
        * jax.nn.sigmoid(npo_beta * (live_total / live_count - ref_logp[0]))
        * seq_len
        / live_count
    )
    grad_out = (npo_weight * mask_f[:, None] * out_grad.astype(jnp.float32)).astype(jnp.bfloat16)
    doc_low = doc_ids.astype(jnp.bfloat16)
    key_nope = jnp.dot(latent, full_uk, preferred_element_type=jnp.float32).astype(jnp.bfloat16)
    values = jnp.dot(latent, full_uv, preferred_element_type=jnp.float32).astype(jnp.bfloat16)
    nope_list, value_list, rope_list, doc_list, latent_list = ([], [], [], [], [])
    for distance in (2, 1):
        far_nope, far_values, far_rope, far_docs = shifted(
            (key_nope, values, k_rope, doc_low), "ctx", distance
        )
        nope_list.append(far_nope)
        value_list.append(far_values)
        rope_list.append(far_rope)
        doc_list.append(far_docs.astype(jnp.float32))
    window_nope = jnp.concatenate(nope_list + [key_nope], axis=0)
    window_value = jnp.concatenate(value_list + [values], axis=0)
    window_rope = jnp.concatenate(rope_list + [k_rope], axis=0)
    window_docs = jnp.concatenate(doc_list + [doc_ids.astype(jnp.float32)], axis=0)
    query_idx = jnp.arange(block_rows, dtype=jnp.int32)
    key_idx = jnp.arange(3 * block_rows, dtype=jnp.int32)
    key_valid = position * block_rows + key_idx - 2 * block_rows >= 0
    allowed = window_docs[None, :] == doc_ids.astype(jnp.float32)[:, None]
    allowed = (
        allowed & (key_idx[None, :] - 2 * block_rows <= query_idx[:, None]) & key_valid[None, :]
    )

    def one_head(inputs):
        head_qn, head_qr, head_kn, head_v, head_g = inputs
        return attend_head(head_qn, head_qr, head_kn, window_rope, head_v, head_g, allowed)

    head_inputs = (
        head_major(q_nope, block_rows, head_count, NOPE),
        head_major(q_rope, block_rows, head_count, ROPE),
        head_major(window_nope, 3 * block_rows, head_count, NOPE),
        head_major(window_value, 3 * block_rows, head_count, VDIM),
        head_major(grad_out, block_rows, head_count, VDIM),
    )
    dq_heads, dqr_heads, nope_heads, value_heads, rope_heads = lax.map(one_head, head_inputs)
    dq_nope = row_major(dq_heads, block_rows, head_count, NOPE)
    dq_rope = row_major(dqr_heads, block_rows, head_count, ROPE)
    part_nope = row_major(nope_heads, 3 * block_rows, head_count, NOPE)
    part_value = row_major(value_heads, 3 * block_rows, head_count, VDIM)
    part_rope = jnp.sum(rope_heads, axis=0).astype(jnp.bfloat16)

    def piece(array, slot_index):
        return array[slot_index * block_rows : (slot_index + 1) * block_rows]

    own_nope = piece(part_nope, 2)
    own_value = piece(part_value, 2)
    rope_total = piece(part_rope, 2).astype(jnp.float32)
    nope_sum = own_nope.astype(jnp.float32)
    value_sum = own_value.astype(jnp.float32)
    for distance in (2, 1):
        slot_index = 2 - distance
        back_nope, back_value, back_rope = shifted(
            (
                piece(part_nope, slot_index),
                piece(part_value, slot_index),
                piece(part_rope, slot_index),
            ),
            "ctx",
            -distance,
        )
        nope_sum = nope_sum + back_nope.astype(jnp.float32)
        value_sum = value_sum + back_value.astype(jnp.float32)
        rope_total = rope_total + back_rope.astype(jnp.float32)
    latent_total = jnp.einsum("tf,lf->tl", nope_sum, full_uk.astype(jnp.float32), precision=highest)
    latent_total = latent_total + jnp.einsum(
        "tf,lf->tl", value_sum, full_uv.astype(jnp.float32), precision=highest
    )
    grad_rows = jnp.concatenate([nope_sum, value_sum], axis=1)
    latent_total, rope_total = (
        lax.psum(latent_total.astype(jnp.bfloat16), "dp").astype(jnp.float32),
        lax.psum(rope_total.astype(jnp.bfloat16), "dp").astype(jnp.float32),
    )
    latent_cols = latent.astype(jnp.float32)
    weight_share = lax.psum_scatter(
        jnp.einsum("tl,tf->lf", latent_cols, grad_rows, precision=highest).astype(jnp.bfloat16),
        "ctx",
        scatter_dimension=0,
        tiled=True,
    ).astype(jnp.float32)
    return (
        dq_nope,
        dq_rope,
        latent_total.astype(jnp.bfloat16),
        rope_total.astype(jnp.bfloat16),
        weight_share[:, :width_nope],
        weight_share[:, width_nope:],
    )


def solution(mesh):
    in_specs = (
        P("ctx", "dp"),
        P("ctx", "dp"),
        P("ctx", None),
        P("ctx", None),
        P("ctx", "dp"),
        P("ctx", "dp"),
        P("ctx", "dp"),
        P("ctx"),
        P(),
        P("ctx"),
        P("ctx"),
    )
    out_specs = (
        P("ctx", "dp"),
        P("ctx", "dp"),
        P("ctx", None),
        P("ctx", None),
        P("ctx", "dp"),
        P("ctx", "dp"),
    )
    return jax.shard_map(
        on_device, mesh=mesh, in_specs=in_specs, out_specs=out_specs, check_vma=False
    )
```

profile of v0, /device:TPU:1, one launch (start us, length us, event | category | flops | bytes accessed | tf_op | source)
XLA Modules:
  0.0 481.2 jit_solution(12793452332927766226)
XLA Ops:
  9.5 4.9 %collective-permute-start.5 = (bf16[128]{0:T(256)(128)(2,1)S(1)}, bf16[128]{0:T(256)(128)(2,1)S(1)}, u32[]{:S(2)}, u32[]{:S(2)}) collective-permute-start(bf16[128]{0:T(256)(128)(2,1)S(1)} %get-tuple-element.220), channel_id=1, source_target_pairs={{0,16},{16,32},{32,48},{48,64},{64,80},{80,96},{96,112},{112,128},... | collective-permute-start | bytes 776 | tf_op jit(solution)/shard_map/ppermute | solution.py:19
  14.4 3.5 collective-permute-start.4
  17.9 0.8 copy.46
  18.8 2.2 collective-permute-start.3
  21.0 3.5 collective-permute-start.2
  24.5 1.3 convert_reduce_fusion
  25.8 46.3 %all-reduce = (f32[]{:T(128)}, f32[]{:T(128)}) all-reduce(f32[]{:T(128)} %get-tuple-element.171, f32[]{:T(128)} %get-tuple-element.170), channel_id=1, replica_groups=mesh['ctx'=32,'dp'=16] {'ctx'}, use_global_device_ids=true, to_apply=%region_1.0 | all-reduce | flops 2 | bytes 16 | tf_op jit(solution)/shard_map/psum | solution.py:73
  75.6 1.1 multiply_convert_fusion
  76.7 1.7 copy.45
  78.7 7.9 %all-gather.3.cloned.1.call-done = bf16[512,1024]{1,0:T(8,128)(2,1)} async-done(((bf16[16,1024]{1,0:T(8,128)(2,1)}), bf16[512,1024]{1,0:T(8,128)(2,1)}) %all-gather.3.cloned.1.call-update) | async-done | bytes 1048592 | tf_op jit(solution)/shard_map/all_gather | solution.py:69
  86.6 1.5 convolution_convert_fusion.6
  88.1 3.1 collective-permute-start.1
  91.3 2.3 collective-permute-start
  93.6 62.9 %all-gather.5.cloned.1.call-done = bf16[512,1024]{1,0:T(8,128)(2,1)} async-done(((bf16[16,1024]{1,0:T(8,128)(2,1)}), bf16[512,1024]{1,0:T(8,128)(2,1)}) %all-gather.5.cloned.1.call-update) | async-done | bytes 1048592 | tf_op jit(solution)/shard_map/all_gather | solution.py:70
  156.5 1.5 convolution_convert_fusion.5
  158.0 3.2 collective-permute-start.7
  161.2 2.3 collective-permute-start.6
  164.5 5.6 %collective-permute-done.6 = bf16[128,1024]{1,0:T(8,128)(2,1)S(1)} collective-permute-done((bf16[128,1024]{1,0:T(8,128)(2,1)S(1)}, bf16[128,1024]{1,0:T(8,128)(2,1)S(1)}, u32[]{:S(2)}, u32[]{:S(2)}) %collective-permute-start.6) | collective-permute-done | bytes 262176 | tf_op jit(solution)/shard_map/ppermute | solution.py:19
  170.3 52.5 %while.19 = (s32[]{:T(128)}, bf16[8,128,128]{2,1,0:T(8,128)(2,1)}, bf16[8,128,64]{1,2,0:T(8,128)(2,1)}, bf16[8,384,128]{1,2,0:T(8,128)(2,1)}, bf16[8,384,128]{1,...) while((s32[]{:T(128)}, bf16[8,128,128]{2,1,0:T(8,128)(2,1)}, ...), condition=%wide.region_8.9_spmd.clone, body=%wide.region_4.8_spmd.clone.sunk | while | flops 95919744 | bytes 4101561 | solution.py:117
  170.3 0.9 fusion.124
  173.1 0.8 fusion.131
  174.7 1.5 fusion.134
  176.8 0.9 fusion.124
  179.6 0.8 fusion.131
  181.2 1.5 fusion.134
  183.4 0.9 fusion.124
  186.2 0.8 fusion.131
  187.8 1.5 fusion.134
  190.0 0.9 fusion.124
  192.7 0.8 fusion.131
  194.3 1.5 fusion.134
  196.5 0.9 fusion.124
  199.3 0.8 fusion.131
  200.9 1.5 fusion.134
  203.1 0.9 fusion.124
  207.5 1.5 fusion.134
  209.6 0.9 fusion.124
  212.4 0.8 fusion.131
  214.0 1.5 fusion.134
  216.2 0.9 fusion.124
  220.6 1.5 fusion.134
  222.8 1.2 fusion.59
  224.0 2.3 collective-permute-start.9
  226.2 1.3 collective-permute-start.8
  227.8 1.9 collective-permute-start.11
  229.7 1.3 collective-permute-start.10
  231.0 2.4 collective-permute-done.9
  233.4 3.9 collective-permute-done.8
  237.4 6.2 %collective-permute-done.11 = bf16[128,1024]{0,1:T(8,128)(2,1)S(1)} collective-permute-done((bf16[128,1024]{0,1:T(8,128)(2,1)S(1)}, bf16[128,1024]{0,1:T(8,128)(2,1)S(1)}, u32[]{:S(2)}, u32[]{:S(2)}) %collective-permute-start.11) | collective-permute-done | bytes 262176 | tf_op jit(solution)/shard_map/ppermute | solution.py:19
  243.7 1.8 fusion.50
  245.5 2.4 copy.59
  248.0 1.1 copy-done.3
  249.8 1.4 fusion.62
  251.2 1.3 collective-permute-start.12
  252.5 5.4 %collective-permute-start.13 = (bf16[128,64]{0,1:T(8,128)(2,1)}, bf16[128,64]{0,1:T(8,128)(2,1)}, u32[]{:S(2)}, u32[]{:S(2)}) collective-permute-start(bf16[128,64]{0,1:T(8,128)(2,1)} %get-tuple-element.219), channel_id=1, source_target_pairs={{16,0},{32,16},{48,32},{64,48},{80,64},{96,80},{112,96},{128,112},... | collective-permute-start | bytes 49160 | tf_op jit(solution)/shard_map/ppermute | solution.py:19
  258.6 1.7 copy.56
  260.3 1.6 collective-permute-done.13
  262.6 60.6 %psum.31 = bf16[128,64]{0,1:T(8,128)(2,1)} all-reduce(bf16[128,64]{0,1:T(8,128)(2,1)S(1)} %add_convert_fusion), channel_id=1, replica_groups=mesh['ctx'=32,'dp'=16] {'dp'}, use_global_device_ids=true, to_apply=%region_11.12 | all-reduce | flops 8192 | bytes 32768 | tf_op jit(solution)/shard_map/psum | solution.py:153
  323.2 1.2 fusion.64
  324.4 1.9 fusion.51
  326.3 31.2 %reduce-scatter.4.cloned.1.call-done = bf16[16,2048]{1,0:T(8,128)(2,1)} async-done(((bf16[512,2048]{1,0:T(8,128)(2,1)}), bf16[16,2048]{1,0:T(8,128)(2,1)}) %reduce-scatter.4.cloned.1.call-update) | async-done | bytes 65552
  357.6 1.1 copy.60
  360.4 112.7 %all-reduce.3.cloned.1.call-done = bf16[128,512]{1,0:T(8,128)(2,1)} async-done(((bf16[128,512]{1,0:T(8,128)(2,1)}), bf16[128,512]{1,0:T(8,128)(2,1)}) %all-reduce.3.cloned.1.call-update) | async-done | bytes 131088 | tf_op jit(solution)/shard_map/psum | solution.py:152
  473.1 1.6 copy.104
  (144 shorter events, 36.5 us)
Async XLA Ops:
  7.2 79.4 %copy-start = (bf16[128,512]{1,0:T(8,128)(2,1)S(1)}, bf16[128,512]{1,0:T(8,128)(2,1)}, u32[]{:S(2)}) copy-start(bf16[128,512]{1,0:T(8,128)(2,1)} %param.15) | copy-start | bytes 393220
  7.2 71.3 %copy-start.4 = (bf16[128,1024]{1,0:T(8,128)(2,1)S(1)}, bf16[128,1024]{1,0:T(8,128)(2,1)}, u32[]{:S(2)}) copy-start(bf16[128,1024]{1,0:T(8,128)(2,1)} %param.13) | copy-start | bytes 786436
  7.2 79.4 %all-gather.3.cloned.1.call-start = ((), (), s32[]{:S(2)}) async-start(), calls=%async_computation.1 | async-start | bytes 1081344 | tf_op jit(solution)/shard_map/all_gather | solution.py:69
  7.9 148.5 %all-gather.5.cloned.1.call-start = ((), (), s32[]{:S(2)}) async-start(), calls=%async_computation.2 | async-start | bytes 1081344 | tf_op jit(solution)/shard_map/all_gather | solution.py:70
  8.7 348.9 %reduce-scatter.4.cloned.1.call-start = ((), (), s32[]{:S(2)}) async-start(), calls=%async_computation.4 | async-start | bytes 2162688
  9.5 69.2 %collective-permute-start.5 = (bf16[128]{0:T(256)(128)(2,1)S(1)}, bf16[128]{0:T(256)(128)(2,1)S(1)}, u32[]{:S(2)}, u32[]{:S(2)}) collective-permute-start(bf16[128]{0:T(256)(128)(2,1)S(1)} %get-tuple-element.220), channel_id=1, source_target_pairs={{0,16},{16,32},{32,48},{48,64},{64,80},{80,96},{96,112},{112,128},... | collective-permute-start | bytes 776 | tf_op jit(solution)/shard_map/ppermute | solution.py:19
  14.4 64.3 %collective-permute-start.4 = (bf16[128]{0:T(256)(128)(2,1)S(1)}, bf16[128]{0:T(256)(128)(2,1)S(1)}, u32[]{:S(2)}, u32[]{:S(2)}) collective-permute-start(bf16[128]{0:T(256)(128)(2,1)S(1)} %get-tuple-element.220), channel_id=1, source_target_pairs={{0,32},{16,48},{32,64},{48,80},{64,96},{80,112},{96,128},{112,144}... | collective-permute-start | bytes 776 | tf_op jit(solution)/shard_map/ppermute | solution.py:19
  18.8 142.4 %collective-permute-start.3 = (bf16[128,64]{1,0:T(8,128)(2,1)S(1)}, bf16[128,64]{1,0:T(8,128)(2,1)S(1)}, u32[]{:S(2)}, u32[]{:S(2)}) collective-permute-start(bf16[128,64]{1,0:T(8,128)(2,1)S(1)} %copy.46), channel_id=1, source_target_pairs={{0,16},{16,32},{32,48},{48,64},{64,80},{80,96},{96,112},{112,128},... | collective-permute-start | bytes 49160 | tf_op jit(solution)/shard_map/ppermute | solution.py:19
  21.0 142.5 %collective-permute-start.2 = (bf16[128,64]{1,0:T(8,128)(2,1)S(1)}, bf16[128,64]{1,0:T(8,128)(2,1)S(1)}, u32[]{:S(2)}, u32[]{:S(2)}) collective-permute-start(bf16[128,64]{1,0:T(8,128)(2,1)S(1)} %copy.46), channel_id=1, source_target_pairs={{0,32},{16,48},{32,64},{48,80},{64,96},{80,112},{96,128},{112,144}... | collective-permute-start | bytes 49160 | tf_op jit(solution)/shard_map/ppermute | solution.py:19
  88.1 75.4 %collective-permute-start.1 = (bf16[128,1024]{1,0:T(8,128)(2,1)S(1)}, bf16[128,1024]{1,0:T(8,128)(2,1)S(1)}, u32[]{:S(2)}, u32[]{:S(2)}) collective-permute-start(bf16[128,1024]{1,0:T(8,128)(2,1)S(1)} %convolution_convert_fusion.6), channel_id=1, source_target_pairs={{0,16},{16,32},{32,48},{48,64},{64,80},{80,96},{96,112},{112,128},... | collective-permute-start | bytes 786440 | tf_op jit(solution)/shard_map/ppermute | solution.py:19
  91.3 72.3 %collective-permute-start = (bf16[128,1024]{1,0:T(8,128)(2,1)S(1)}, bf16[128,1024]{1,0:T(8,128)(2,1)S(1)}, u32[]{:S(2)}, u32[]{:S(2)}) collective-permute-start(bf16[128,1024]{1,0:T(8,128)(2,1)S(1)} %convolution_convert_fusion.6), channel_id=1, source_target_pairs={{0,32},{16,48},{32,64},{48,80},{64,96},{80,112},{96,128},{112,144}... | collective-permute-start | bytes 786440 | tf_op jit(solution)/shard_map/ppermute | solution.py:19
  158.0 6.5 %collective-permute-start.7 = (bf16[128,1024]{1,0:T(8,128)(2,1)S(1)}, bf16[128,1024]{1,0:T(8,128)(2,1)S(1)}, u32[]{:S(2)}, u32[]{:S(2)}) collective-permute-start(bf16[128,1024]{1,0:T(8,128)(2,1)S(1)} %convolution_convert_fusion.5), channel_id=1, source_target_pairs={{0,16},{16,32},{32,48},{48,64},{64,80},{80,96},{96,112},{112,128},... | collective-permute-start | bytes 786440 | tf_op jit(solution)/shard_map/ppermute | solution.py:19
  161.2 8.9 %collective-permute-start.6 = (bf16[128,1024]{1,0:T(8,128)(2,1)S(1)}, bf16[128,1024]{1,0:T(8,128)(2,1)S(1)}, u32[]{:S(2)}, u32[]{:S(2)}) collective-permute-start(bf16[128,1024]{1,0:T(8,128)(2,1)S(1)} %convolution_convert_fusion.5), channel_id=1, source_target_pairs={{0,32},{16,48},{32,64},{48,80},{64,96},{80,112},{96,128},{112,144}... | collective-permute-start | bytes 786440 | tf_op jit(solution)/shard_map/ppermute | solution.py:19
  224.0 9.4 %collective-permute-start.9 = (bf16[128,1024]{0,1:T(8,128)(2,1)S(1)}, bf16[128,1024]{0,1:T(8,128)(2,1)S(1)}, u32[]{:S(2)}, u32[]{:S(2)}) collective-permute-start(bf16[128,1024]{0,1:T(8,128)(2,1)S(1)} %bitcast.164), channel_id=1, source_target_pairs={{16,0},{32,16},{48,32},{64,48},{80,64},{96,80},{112,96},{128,112},... | collective-permute-start | bytes 786440 | tf_op jit(solution)/shard_map/ppermute | solution.py:19
  226.2 11.0 %collective-permute-start.8 = (bf16[128,1024]{0,1:T(8,128)(2,1)S(1)}, bf16[128,1024]{0,1:T(8,128)(2,1)S(1)}, u32[]{:S(2)}, u32[]{:S(2)}) collective-permute-start(bf16[128,1024]{0,1:T(8,128)(2,1)S(1)} %bitcast.162), channel_id=1, source_target_pairs={{32,0},{48,16},{64,32},{80,48},{96,64},{112,80},{128,96},{144,112}... | collective-permute-start | bytes 786440 | tf_op jit(solution)/shard_map/ppermute | solution.py:19
  227.8 15.8 %collective-permute-start.11 = (bf16[128,1024]{0,1:T(8,128)(2,1)S(1)}, bf16[128,1024]{0,1:T(8,128)(2,1)S(1)}, u32[]{:S(2)}, u32[]{:S(2)}) collective-permute-start(bf16[128,1024]{0,1:T(8,128)(2,1)S(1)} %bitcast.165), channel_id=1, source_target_pairs={{16,0},{32,16},{48,32},{64,48},{80,64},{96,80},{112,96},{128,112},... | collective-permute-start | bytes 786440 | tf_op jit(solution)/shard_map/ppermute | solution.py:19
  229.7 13.9 %collective-permute-start.10 = (bf16[128,1024]{0,1:T(8,128)(2,1)S(1)}, bf16[128,1024]{0,1:T(8,128)(2,1)S(1)}, u32[]{:S(2)}, u32[]{:S(2)}) collective-permute-start(bf16[128,1024]{0,1:T(8,128)(2,1)S(1)} %bitcast.163), channel_id=1, source_target_pairs={{32,0},{48,16},{64,32},{80,48},{96,64},{112,80},{128,96},{144,112}... | collective-permute-start | bytes 786440 | tf_op jit(solution)/shard_map/ppermute | solution.py:19
  248.0 1.1 copy-start.3
  248.0 9.9 %copy-start.5 = (bf16[8,128,128]{2,1,0:T(8,128)(2,1)S(1)}, bf16[8,128,128]{2,1,0:T(8,128)(2,1)}, u32[]{:S(2)}) copy-start(bf16[8,128,128]{2,1,0:T(8,128)(2,1)} %get-tuple-element.77) | copy-start | bytes 786436
  248.0 75.2 %copy-start.1 = (bf16[512,1024]{1,0:T(8,128)(2,1)S(1)}, bf16[512,1024]{1,0:T(8,128)(2,1)}, u32[]{:S(2)}) copy-start(bf16[512,1024]{1,0:T(8,128)(2,1)} %all-gather.5.cloned.1.call-done) | copy-start | bytes 3145732
  248.0 225.1 %all-reduce.3.cloned.1.call-start = ((), (), s32[]{:S(2)}) async-start(), calls=%async_computation.3 | async-start | bytes 262144 | tf_op jit(solution)/shard_map/psum | solution.py:152
  249.8 74.7 %copy-start.2 = (bf16[512,1024]{1,0:T(8,128)(2,1)S(1)}, bf16[512,1024]{1,0:T(8,128)(2,1)}, u32[]{:S(2)}) copy-start(bf16[512,1024]{1,0:T(8,128)(2,1)} %all-gather.3.cloned.1.call-done) | copy-start | bytes 3145732
  251.2 9.1 %collective-permute-start.12 = (bf16[128,64]{0,1:T(8,128)(2,1)}, bf16[128,64]{0,1:T(8,128)(2,1)S(1)}, u32[]{:S(2)}, u32[]{:S(2)}) collective-permute-start(bf16[128,64]{0,1:T(8,128)(2,1)} %get-tuple-element.218), channel_id=1, source_target_pairs={{32,0},{48,16},{64,32},{80,48},{96,64},{112,80},{128,96},{144,112}... | collective-permute-start | bytes 49160 | tf_op jit(solution)/shard_map/ppermute | solution.py:19
  252.5 9.4 %collective-permute-start.13 = (bf16[128,64]{0,1:T(8,128)(2,1)}, bf16[128,64]{0,1:T(8,128)(2,1)}, u32[]{:S(2)}, u32[]{:S(2)}) collective-permute-start(bf16[128,64]{0,1:T(8,128)(2,1)} %get-tuple-element.219), channel_id=1, source_target_pairs={{16,0},{32,16},{48,32},{64,48},{80,64},{96,80},{112,96},{128,112},... | collective-permute-start | bytes 49160 | tf_op jit(solution)/shard_map/ppermute | solution.py:19
Sparse Core Ops, SparseCore 0:
  10.1 76.4 all-gather.2
  88.7 67.6 all-gather.4
  248.1 109.4 reduce-scatter.3
  361.5 111.5 all-reduce.2
where the time goes:
time: 484 us; the launch traced here: 481 us
  waiting for transfers between devices  237 us (49%)
  blocking collectives  107 us (22%)
  matrix products  49.9 us (10%)
  starting transfers between devices  38.7 us (8%)
  local copies, waits for them, and re-layouts  23.2 us (5%)
  between operations  16.9 us (3%)
  other arithmetic  8.61 us (2%)
    psum x1, waiting for transfers between devices, on_device(): lax.psum(latent_total.astype(jnp.bfloat16), 'dp').astype(jnp.float32)  113 us
    all_gather x1, waiting for transfers between devices, on_device(): lax.all_gather(w_uv, 'ctx', axis=0, tiled=True)  62.9 us
    psum x1, blocking collectives, on_device(): lax.psum(rope_total.astype(jnp.bfloat16), 'dp').astype(jnp.float32)  60.6 us
    psum x1, blocking collectives, on_device(): lax.psum((jnp.sum(mask_f * log_prob), jnp.sum(mask_f)), 'ctx')  46.3 us
    ppermute x14, starting transfers between devices, shifted(): return lax.ppermute(block, axis, route)  38.6 us
    unnamed x5, waiting for transfers between devices  32.6 us
    ppermute x14, waiting for transfers between devices, shifted(): return lax.ppermute(block, axis, route)  20.5 us
    unnamed x21, local copies, waits for them, and re-layouts  12.1 us
  transfers between devices with their start and end apart: 18, of which 10 were waited for; matrix products, arithmetic and copies ran while one was open for 4% of the time, Pallas kernels for 0%

commit v1 on v0

v1 whole, which is shorter than its diff:
```python
import math

import jax
import jax.numpy as jnp
from jax import lax
from jax.experimental import pallas as pl
from jax.experimental.pallas import tpu as pltpu
from jax.sharding import PartitionSpec as P

NOPE = 128
ROPE = 64
npo_beta = 1.0
MESH = pl.DeviceIdType.MESH
RIGHT = (8, 7, 8)
LEFT = (7, 8, 7)
VMEM = pl.BlockSpec(memory_space=pltpu.VMEM)
f32 = jnp.float32
bf16 = jnp.bfloat16


def greet(peers):
    barrier = pltpu.get_barrier_semaphore()
    for peer in peers:
        pl.semaphore_signal(barrier, inc=1, device_id=peer, device_id_type=MESH)
    pl.semaphore_wait(barrier, len(peers))


def remote(src, dst, send, recv, peer):
    return pltpu.make_async_remote_copy(
        src_ref=src, dst_ref=dst, send_sem=send, recv_sem=recv, device_id=peer, device_id_type=MESH
    )


def loop(first, last, body):
    def step(s, carry):
        body(s)
        return carry

    lax.fori_loop(first, last, step, 0)


def gather_kernel(
    uk_ref, uv_ref, st_ref, h_ref, buk, buv, bst, win,
    own_sem, ring_send, ring_recv, par_send, par_recv, halo_send, halo_recv,
):
    me = lax.axis_index("ctx")
    n = 32
    right, left = lax.rem(me + 2, n), lax.rem(me + n - 2, n)
    partner = me + 1 - 2 * lax.rem(me, 2)
    ring_peer = ({"ctx": right}, {"ctx": left})
    mate = {"ctx": partner}
    near = {"ctx": lax.rem(me + 1, n)}
    srcs, bufs = (uk_ref, uv_ref, st_ref), (buk, buv, bst)
    counts = (RIGHT, LEFT)

    def index(base, way, s):
        return lax.rem(base + n - 2 * s, n) if way == 0 else lax.rem(base + 2 * s, n)

    def ring(i, way, s):
        slot = bufs[i].at[index(me, way, s)]
        src = srcs[i] if isinstance(s, int) and s == 0 else slot
        return remote(src, slot, ring_send.at[i, way, s], ring_recv.at[i, way, s], ring_peer[way])

    def arrival(i, way, s):
        slot = bufs[i].at[index(me, way, s)]
        return remote(slot, slot, ring_send.at[i, way, s - 1], ring_recv.at[i, way, s - 1], ring_peer[way])

    def mate_copy(i, way, s, base):
        slot = bufs[i].at[index(base, way, s)]
        src = srcs[i] if isinstance(s, int) and s == 0 else slot
        return remote(src, slot, par_send.at[i, way, s], par_recv.at[i, way, s], mate)

    halo = [
        remote(h_ref, win.at[1], halo_send.at[0], halo_recv.at[0], near),
        remote(h_ref, win.at[0], halo_send.at[1], halo_recv.at[1], ring_peer[0]),
    ]
    own = [pltpu.make_async_copy(srcs[i], bufs[i].at[me], own_sem.at[i]) for i in range(3)]
    own.append(pltpu.make_async_copy(h_ref, win.at[2], own_sem.at[3]))

    greet([{"ctx": lax.rem(me + d, n)} for d in (1, 2, n - 1, n - 2)])
    for i in range(3):
        for way in range(2):
            ring(i, way, 0).start()
    for i in range(3):
        mate_copy(i, 0, 0, me).start()
    for copy in own:
        copy.start()

    def middle(s):
        for i in range(3):
            for way in range(2):
                arrival(i, way, s).wait_recv()
                ring(i, way, s).start()
                mate_copy(i, way, s, me).start()

    loop(1, 3, middle)
    for copy in halo:
        copy.start()
    loop(3, 7, middle)
    for s in (7, 8):
        for i in range(3):
            for way in range(2):
                if s <= counts[way][i]:
                    arrival(i, way, s).wait_recv()
                    if s < counts[way][i]:
                        ring(i, way, s).start()
                    mate_copy(i, way, s, me).start()

    for copy in own:
        copy.wait()
    for copy in halo:
        copy.wait_send()
        copy.wait_recv()

    def settle(s):
        for i in range(3):
            for way in range(2):
                ring(i, way, s).wait_send()
                mate_copy(i, way, s, me).wait_send()
                mate_copy(i, way, s, partner).wait_recv()

    for i in range(3):
        for way in range(2):
            ring(i, way, 0).wait_send()
        mate_copy(i, 0, 0, me).wait_send()
        mate_copy(i, 0, 0, partner).wait_recv()
    loop(1, 7, settle)
    for s in (7, 8):
        for i in range(3):
            for way in range(2):
                if s <= counts[way][i]:
                    if s < counts[way][i]:
                        ring(i, way, s).wait_send()
                    mate_copy(i, way, s, me).wait_send()
                    mate_copy(i, way, s, partner).wait_recv()


def gather(uk, uv, stats, halo):
    sem = pltpu.SemaphoreType.DMA
    return pl.pallas_call(
        gather_kernel,
        out_shape=(
            jax.ShapeDtypeStruct((32,) + uk.shape, bf16),
            jax.ShapeDtypeStruct((32,) + uv.shape, bf16),
            jax.ShapeDtypeStruct((32,) + stats.shape, f32),
            jax.ShapeDtypeStruct((3,) + halo.shape, bf16),
        ),
        in_specs=[VMEM] * 4,
        out_specs=(VMEM,) * 4,
        scratch_shapes=[
            sem((4,)), sem((3, 2, 8)), sem((3, 2, 8)), sem((3, 2, 9)), sem((3, 2, 9)), sem((2,)), sem((2,)),
        ],
        compiler_params=pltpu.CompilerParams(collective_id=0, has_side_effects=True),
    )(uk, uv, stats, halo)


def dot_nt(a, b):
    return lax.dot_general(a, b, (((1,), (1,)), ((), ())), preferred_element_type=f32)


def dot_tn(a, b):
    return lax.dot_general(a, b, (((0,), (0,)), ((), ())), preferred_element_type=f32)


def dot_nn(a, b):
    return jnp.dot(a, b, preferred_element_type=f32)


def attend_kernel(
    pos_ref, logp_ref, win_ref, uk_ref, uv_ref, q_ref, qr_ref, og_ref, st_ref, mask_ref, doc_ref,
    dq_ref, dqr_ref, dwk_ref, dwv_ref, dl_ref, acc, lat_t, gscale,
):
    step = pl.program_id(0)
    latent = win_ref[:, :512]

    @pl.when(step == 0)
    def _():
        acc[...] = jnp.zeros_like(acc)
        lat_t[...] = latent.astype(f32).T.astype(bf16)
        sums = jnp.sum(jnp.sum(st_ref[...], axis=0), axis=1, keepdims=True)
        live_total, live_count = sums[0:1], sums[1:2]
        gap = npo_beta * (live_total / live_count - logp_ref[0])
        weight = 2.0 * (1.0 / (1.0 + jnp.exp(-gap))) * 4096.0 / live_count
        gscale[...] = weight * mask_ref[...]

    scale = 1.0 / math.sqrt(NOPE + ROPE)
    key_idx = lax.broadcasted_iota(jnp.int32, (384, 128), 0) - 256
    query_idx = lax.broadcasted_iota(jnp.int32, (384, 128), 1)
    allowed = win_ref[:, 640:768].astype(f32) == doc_ref[...]
    allowed = allowed & (key_idx <= query_idx) & (pos_ref[0] * 128 + key_idx >= 0)
    low_lane = lax.broadcasted_iota(jnp.int32, (128, 128), 1) < ROPE
    keys = dot_nn(latent, uk_ref[...]).astype(bf16)
    values = dot_nn(latent, uv_ref[...]).astype(bf16)
    key_rope = win_ref[:, 512:640]
    query_rope = qr_ref[...].astype(f32)
    scale_col = gscale[...]
    part_k, part_v, rope_q, rope_k = [], [], [], 0.0
    for p in range(2):
        cols = slice(p * 128, p * 128 + 128)
        qn = q_ref[:, cols]
        mine = low_lane if p == 0 else jnp.logical_not(low_lane)
        qr = jnp.where(mine, query_rope, 0.0).astype(bf16)
        kh, vh = keys[:, cols], values[:, cols]
        grad = (scale_col * og_ref[:, cols].astype(f32)).astype(bf16)
        scores = dot_nt(kh, qn) + dot_nt(key_rope, qr)
        scores = jnp.where(allowed, scores * scale, -1e30)
        top = jnp.max(scores, axis=0, keepdims=True)
        expon = jnp.where(allowed, jnp.exp(scores - top), 0.0)
        probs = expon * (1.0 / jnp.sum(expon, axis=0, keepdims=True))
        low = probs.astype(bf16)
        dprob = dot_nt(vh, grad)
        delta = jnp.sum(low.astype(f32) * dprob, axis=0, keepdims=True)
        dscore = (probs * (dprob - delta) * scale).astype(bf16)
        dq_ref[:, cols] = dot_tn(dscore, kh).astype(bf16)
        rope_q.append(dot_tn(dscore, key_rope))
        rope_k = rope_k + dot_nn(dscore, qr)
        part_k.append(dot_nn(dscore, qn).astype(bf16))
        part_v.append(dot_nn(low, grad).astype(bf16))
    dqr_ref[...] = jnp.where(low_lane, rope_q[0], rope_q[1]).astype(bf16)
    part_k = jnp.concatenate(part_k, axis=1)
    part_v = jnp.concatenate(part_v, axis=1)
    acc[:, :512] += dot_nt(part_k, uk_ref[...]) + dot_nt(part_v, uv_ref[...])
    acc[:, 512:] += rope_k
    dwk_ref[...] = dot_nn(lat_t[...], part_k).astype(bf16)
    dwv_ref[...] = dot_nn(lat_t[...], part_v).astype(bf16)

    @pl.when(step == pl.num_programs(0) - 1)
    def _():
        dl_ref[...] = acc[...].astype(bf16)


def attend(position, ref_logp, window, uk, uv, q_nope, q_rope, out_grad, stats, mask_col, doc_row):
    width = uk.shape[1]

    def cols(rows, block):
        return pl.BlockSpec((rows, block), lambda i: (0, i))

    def whole(shape):
        return pl.BlockSpec(shape, lambda i: (0,) * len(shape))

    scalar = pl.BlockSpec(memory_space=pltpu.SMEM)
    return pl.pallas_call(
        attend_kernel,
        grid=(width // 256,),
        out_shape=(
            jax.ShapeDtypeStruct(q_nope.shape, bf16),
            jax.ShapeDtypeStruct(q_rope.shape, bf16),
            jax.ShapeDtypeStruct((512, width), bf16),
            jax.ShapeDtypeStruct((512, width), bf16),
            jax.ShapeDtypeStruct((384, 640), bf16),
        ),
        in_specs=[
            scalar, scalar, whole((384, 768)), cols(512, 256), cols(512, 256), cols(128, 256),
            cols(128, 128), cols(128, 256), whole(stats.shape), whole((128, 1)), whole((1, 128)),
        ],
        out_specs=(cols(128, 256), cols(128, 128), cols(512, 256), cols(512, 256), whole((384, 640))),
        scratch_shapes=[
            pltpu.VMEM((384, 640), f32), pltpu.VMEM((512, 384), bf16), pltpu.VMEM((128, 1), f32),
        ],
        compiler_params=pltpu.CompilerParams(dimension_semantics=("arbitrary",)),
    )(position, ref_logp, window, uk, uv, q_nope, q_rope, out_grad, stats, mask_col, doc_row)


def reduce_kernel(
    dwk, dwv, dl, ok, ov, olat, orope, par_buf, recv_buf, send_buf, back, mix, inbox, mine, final,
    par_send, par_recv, ring_send, ring_recv, back_send, back_recv, mix_send, mix_recv, all_send, all_recv,
):
    me, col = lax.axis_index("ctx"), lax.axis_index("dp")
    n, m = 32, 16
    core = lax.rem(me, 2)
    partner = me + 1 - 2 * core
    ring_peer = ({"ctx": lax.rem(me + 2, n)}, {"ctx": lax.rem(me + n - 2, n)})
    mate = {"ctx": partner}
    grads, counts = (dwk, dwv), (RIGHT, LEFT)
    others = [lax.rem(col + k, m) for k in range(1, m)]

    def to_mate(i, d):
        src = grads[i].at[lax.rem(partner + 2 * d, n)]
        return remote(src, par_buf.at[i, d], par_send.at[i, d], par_recv.at[i, d], mate)

    def back_copy(d):
        peer = {"ctx": lax.rem(me + n - d, n)}
        return remote(dl.at[2 - d], back.at[d - 1], back_send.at[d - 1], back_recv.at[d - 1], peer)

    def mix_copy(k):
        return remote(
            mix.at[others[k - 1]], inbox.at[k - 1], mix_send.at[k - 1], mix_recv.at[k - 1],
            {"dp": others[k - 1]},
        )

    def all_copy(k):
        return remote(
            mine, final.at[k], all_send.at[k - 1], all_recv.at[k - 1], {"dp": others[k - 1]}
        )

    def ring(i, way, s):
        return remote(
            send_buf.at[i, way, s], recv_buf.at[i, way, s], ring_send.at[i, way, s],
            ring_recv.at[i, way, s], ring_peer[way],
        )

    def local(i, d):
        to_mate(i, d).wait_recv()
        total = grads[i][lax.rem(me + 2 * d, n)].astype(f32)
        return total + par_buf[i, d].astype(f32)

    greet(
        [{"ctx": lax.rem(me + d, n)} for d in (1, 2, n - 1, n - 2)] + [{"dp": k} for k in others]
    )
    order = (8, 7, 9, 6, 10, 5, 11, 4, 12, 3, 13, 2, 14, 1, 15, 0)
    for d in order[:3]:
        for i in range(2):
            to_mate(i, d).start()
    for d in (2, 1):
        back_copy(d).start()
    for d in order[3:]:
        for i in range(2):
            to_mate(i, d).start()

    def ring_step(i, way, s):
        count = counts[way][i]
        d = count - s if way == 0 else 16 - count + s
        total = local(i, d)
        if not (isinstance(s, int) and s == 0):
            ring(i, way, s - 1).wait_recv()
            total = total + recv_buf[i, way, s - 1].astype(f32)
        send_buf[i, way, s] = total.astype(bf16)
        ring(i, way, s).start()

    def middle(s):
        for i in range(2):
            for way in range(2):
                ring_step(i, way, s)

    middle(0)
    for d in (2, 1):
        back_copy(d).wait_recv()
    summed = dl[2].astype(f32) + back[0].astype(f32) + back[1].astype(f32)
    mix[...] = summed.reshape(16, 8, 640).astype(bf16)
    for k in range(1, m):
        mix_copy(k).start()
    loop(1, 3, middle)
    total = mix[col].astype(f32)
    for k in range(1, m):
        mix_copy(k).wait_recv()
        total = total + inbox[k - 1].astype(f32)
    rope = total[:, 512:]
    rope = rope + pltpu.roll(rope, 64, 1)
    mine[...] = jnp.concatenate([total[:, :512], rope], axis=1).astype(bf16)
    for k in range(1, m):
        all_copy(k).start()
    loop(3, 7, middle)
    for i in range(2):
        for way in range(2):
            if counts[way][i] == 8:
                ring_step(i, way, 7)
    final[0] = mine[...]
    for k in range(1, m):
        all_copy(k).wait_recv()
    for j in range(m):
        rows = final[lax.rem(col + m - j, m)].astype(f32)
        olat[8 * j:8 * j + 8, :] = rows[:, :512].astype(bf16)
        orope[8 * j:8 * j + 8, :] = rows[:, 512:512 + ROPE].astype(bf16)
    outs = (ok, ov)
    for i in range(2):
        total = local(i, 0)
        for way in range(2):
            last = counts[way][i] - 1
            ring(i, way, last).wait_recv()
            total = total + recv_buf[i, way, last].astype(f32)
        outs[i][...] = total
    for i in range(2):
        for d in range(16):
            to_mate(i, d).wait_send()
        for way in range(2):
            for s in range(counts[way][i]):
                ring(i, way, s).wait_send()
    for d in (2, 1):
        back_copy(d).wait_send()
    for k in range(1, m):
        mix_copy(k).wait_send()
        all_copy(k).wait_send()


def reduce(dwk, dwv, dl):
    sem = pltpu.SemaphoreType.DMA
    width = dwk.shape[2]
    return pl.pallas_call(
        reduce_kernel,
        out_shape=(
            jax.ShapeDtypeStruct((16, width), f32),
            jax.ShapeDtypeStruct((16, width), f32),
            jax.ShapeDtypeStruct((128, 512), bf16),
            jax.ShapeDtypeStruct((128, ROPE), bf16),
        ),
        in_specs=[VMEM] * 3,
        out_specs=(VMEM,) * 4,
        scratch_shapes=[
            pltpu.VMEM((2, 16, 16, width), bf16),
            pltpu.VMEM((2, 2, 8, 16, width), bf16),
            pltpu.VMEM((2, 2, 8, 16, width), bf16),
            pltpu.VMEM((2, 128, 640), bf16),
            pltpu.VMEM((16, 8, 640), bf16),
            pltpu.VMEM((15, 8, 640), bf16),
            pltpu.VMEM((8, 640), bf16),
            pltpu.VMEM((16, 8, 640), bf16),
            sem((2, 16)), sem((2, 16)), sem((2, 2, 8)), sem((2, 2, 8)),
            sem((2,)), sem((2,)), sem((15,)), sem((15,)), sem((15,)), sem((15,)),
        ],
        compiler_params=pltpu.CompilerParams(collective_id=1, has_side_effects=True),
    )(dwk, dwv, dl)


def on_device(
    q_nope, q_rope, latent, k_rope, w_uk, w_uv, out_grad, log_prob, ref_logp, doc_ids, loss_mask
):
    mask_f = loss_mask.astype(f32)
    stats = jnp.concatenate(
        [(mask_f * log_prob)[None, :], mask_f[None, :], jnp.zeros((6, 128), f32)], axis=0
    )
    docs = jnp.broadcast_to(doc_ids.astype(bf16)[:, None], (128, 128))
    halo = jnp.concatenate([latent, k_rope, k_rope, docs], axis=1)
    position = lax.axis_index("ctx").astype(jnp.int32).reshape(1)
    full_uk, full_uv, all_stats, window = gather(w_uk, w_uv, stats, halo)
    width = w_uk.shape[1]
    dq_nope, dq_rope, dwk, dwv, dl = attend(
        position, ref_logp, window.reshape(384, 768), full_uk.reshape(512, width),
        full_uv.reshape(512, width), q_nope, q_rope, out_grad, all_stats, mask_f[:, None],
        doc_ids.astype(f32)[None, :],
    )
    dw_uk, dw_uv, d_latent, d_krope = reduce(
        dwk.reshape(32, 16, width), dwv.reshape(32, 16, width), dl.reshape(3, 128, 640)
    )
    return dq_nope, dq_rope, d_latent, d_krope, dw_uk, dw_uv


def solution(mesh):
    both, rows, flat = P("ctx", "dp"), P("ctx", None), P("ctx")
    return jax.shard_map(
        on_device,
        mesh=mesh,
        in_specs=(both, both, rows, rows, both, both, both, flat, P(), flat, flat),
        out_specs=(both, both, rows, rows, both, both),
        check_vma=False,
    )
```

time: 484 us -> 111 us (0.23)
  the two profiles are of different devices: /device:TPU:1 before, /device:TPU:2 now
where the time goes in v1:
time: 111 us
  Pallas kernels  99.2 us (89%)
  local copies, waits for them, and re-layouts  6.28 us (6%)
  other arithmetic  4.01 us (4%)
  between operations  1.37 us (1%)
    pallas_call x1, Pallas kernels, gather(): pl.pallas_call(gather_kernel, out_shape=(jax.ShapeDtypeStruct((32,) + uk....  45.5 us
    pallas_call x1, Pallas kernels, reduce(): pl.pallas_call(reduce_kernel, out_shape=(jax.ShapeDtypeStruct((16, width)...  42.1 us
    pallas_call x1, Pallas kernels, attend(): pl.pallas_call(attend_kernel, grid=(width // 256,), out_shape=(jax.ShapeD...  11.6 us
    unnamed x11, local copies, waits for them, and re-layouts  5.37 us

profile of v1, /device:TPU:2, one launch (start us, length us, event | category | flops | bytes accessed | tf_op | source)
XLA Modules:
  0.0 110.9 jit_solution(2601530423693725075)
XLA Ops:
  0.6 0.0 copy-start
  1.3 0.7 multiply_bitcast_fusion
  2.0 0.1 pad.6.clone
  2.1 1.2 %convert_bitcast_fusion = (f32[1,128]{1,0:T(1,128)}, bf16[128]{0:T(256)(128)(2,1)S(1)}) fusion(s32[128]{0:T(128)} %param.20), kind=kLoop, calls=%fused_computation.2 | loop fusion | flops 256 | bytes 1280 | tf_op jit(solution)/shard_map/broadcast_in_dim | solution.py:429
  3.3 0.7 convert_bitcast_fusion.1
  4.0 0.7 maximum_maximum_fusion.st_ref
  4.6 0.1 broadcast_in_dim.24
  4.7 0.8 copy.17
  5.6 0.8 copy.19.mask_ref
  6.3 0.0 copy-done
  6.3 0.8 pad_maximum_fusion.h_ref
  7.1 45.5 %shard_map.154 = (bf16[32,16,1024]{2,1,0:T(8,128)(2,1)}, bf16[32,16,1024]{2,1,0:T(8,128)(2,1)}, f32[32,8,128]{2,1,0:T(8,128)}, bf16[3,128,768]{2,1,0:T(8,128)(2,1)}) custom-call(bf16[16,1024]{1,0:T(8,128)(2,1)} %uk_ref.1, bf16[16,1024]{1,0:T(8,128)(2,1)} %uv_ref.1, f32[8,128]{1,0:T(8,128)} %maximum_maximum_fusion.st_ref, bf16[128,768]{1,0:T(8,128)(2,1)} %pad_maximum_fusion.h_ref), custom_call_target="tpu_custom_call" | custom-call | tf_op jit(solution)/shard_map/pallas_call | solution.py:140
  52.6 11.6 %shard_map.155 = (bf16[128,1024]{1,0:T(8,128)(2,1)}, bf16[128,512]{1,0:T(8,128)(2,1)}, bf16[512,1024]{1,0:T(8,128)(2,1)}, bf16[512,1024]{1,0:T(8,128)(2,1)}, bf16[384,640]{1,0:T(8,128)(2,1)}) custom-call(s32[1]{0:T(128)} %bitcast.pos_ref, f32[1]{0:T(128)S(6)} %copy.24.logp_ref, bf16[384,768]{1,0:T(8,128)(2,1)} %bitcast.19, bf16[512,1024]{1,0:T(8,128)(2,1)} %bitcast.17, ...), custom_call_target="tpu_custom_call" | custom-call | tf_op jit(solution)/shard_map/pallas_call | solution.py:242
  64.2 42.1 %shard_map.156 = (f32[16,1024]{1,0:T(8,128)}, f32[16,1024]{1,0:T(8,128)}, bf16[128,512]{1,0:T(8,128)(2,1)}, bf16[128,64]{1,0:T(8,128)(2,1)}) custom-call(bf16[32,16,1024]{2,1,0:T(8,128)(2,1)} %bitcast.15, bf16[32,16,1024]{2,1,0:T(8,128)(2,1)} %bitcast.16, bf16[3,128,640]{2,1,0:T(8,128)(2,1)} %bitcast.20), custom_call_target="tpu_custom_call" | custom-call | tf_op jit(solution)/shard_map/pallas_call | solution.py:388
  106.3 1.4 %copy.20 = bf16[128,64]{0,1:T(8,128)(2,1)} copy(bf16[128,64]{1,0:T(8,128)(2,1)} %get-tuple-element.35) | data formatting | bytes 32768
  107.8 0.0 copy-start.2
  107.8 1.6 %copy.25 = bf16[128,512]{1,0:T(8,128)(2,1)} copy(bf16[128,512]{1,0:T(8,128)(2,1)} %get-tuple-element.50) | data formatting | bytes 262144
  109.4 0.0 copy-done.2
  109.4 0.0 copy-start.1
  109.4 0.6 copy.26
  110.0 0.2 copy-done.1
  110.3 0.6 copy.27
  (1 shorter events, 0.0 us)
Async XLA Ops:
  0.6 5.7 %copy-start = (bf16[128,512]{1,0:T(8,128)(2,1)S(1)}, bf16[128,512]{1,0:T(8,128)(2,1)}, u32[]{:S(2)}) copy-start(bf16[128,512]{1,0:T(8,128)(2,1)} %param.13) | copy-start | bytes 393220
  107.8 1.6 %copy-start.2 = (f32[16,1024]{1,0:T(8,128)S(1)}, f32[16,1024]{1,0:T(8,128)}, u32[]{:S(2)}) copy-start(f32[16,1024]{1,0:T(8,128)} %get-tuple-element.52) | copy-start | bytes 196612
  109.4 0.9 copy-start.1

commit v2 on v1

v2 whole, which is shorter than its diff:
```python
import math

import jax
import jax.numpy as jnp
from jax import lax
from jax.experimental import pallas as pl
from jax.experimental.pallas import tpu as pltpu
from jax.sharding import PartitionSpec as P

NOPE = 128
ROPE = 64
npo_beta = 1.0
MESH = pl.DeviceIdType.MESH
VMEM = pl.BlockSpec(memory_space=pltpu.VMEM)
f32 = jnp.float32
bf16 = jnp.bfloat16


def greet(peers):
    barrier = pltpu.get_barrier_semaphore()
    for peer in peers:
        pl.semaphore_signal(barrier, inc=1, device_id=peer, device_id_type=MESH)
    pl.semaphore_wait(barrier, len(peers))


def remote(src, dst, send, recv, peer):
    return pltpu.make_async_remote_copy(
        src_ref=src, dst_ref=dst, send_sem=send, recv_sem=recv, device_id=peer, device_id_type=MESH
    )


def relay(d):
    return 3 * ((d - 1) // 3)


def gather_kernel(
    uk_ref, uv_ref, lat_ref, rope_ref, logp_ref, base_ref, doc_ref, mask_ref,
    buk, buv, bst, win, win_r, tile,
    own_sem, ring_send, ring_recv, par_send, par_recv, halo_send, halo_recv,
):
    me = lax.axis_index("ctx")
    n = 32
    core = lax.rem(me, 2)
    partner = me + 1 - 2 * core
    mate = {"ctx": partner}
    srcs, bufs = (uk_ref, uv_ref, tile), (buk, buv, bst)
    counts = ((7, 7, 8), (8, 8, 7))

    mask = mask_ref[...].astype(f32)
    tile[0:1, :] = mask * logp_ref[...]
    tile[1:2, :] = mask
    tile[2:3, :] = doc_ref[...].astype(f32)
    tile[3:4, :] = jnp.broadcast_to(base_ref[...], (1, 128))
    tile[4:8, :] = jnp.zeros((4, 128), f32)

    def away(way, hops):
        return lax.rem(me + 2 * hops, n) if way == 0 else lax.rem(me + n - 2 * hops, n)

    def origin(base, way, d):
        return lax.rem(base + n - 2 * d, n) if way == 0 else lax.rem(base + 2 * d, n)

    def send(i, way, d):
        slot = bufs[i].at[origin(me, way, relay(d))]
        src = srcs[i] if relay(d) == 0 else slot
        peer = {"ctx": away(way, d - relay(d))}
        return remote(src, slot, ring_send.at[i, way, d], ring_recv.at[i, way, d], peer)

    def arrival(i, way, d):
        slot = bufs[i].at[origin(me, way, d)]
        peer = {"ctx": away(1 - way, d - relay(d))}
        return remote(slot, slot, ring_send.at[i, way, d], ring_recv.at[i, way, d], peer)

    def mate_copy(i, way, d, base):
        slot = bufs[i].at[origin(base, way, d)]
        src = srcs[i] if d == 0 else slot
        return remote(src, slot, par_send.at[i, way, d], par_recv.at[i, way, d], mate)

    next_chip = {"ctx": away(0, 1)}
    halo = [
        remote(lat_ref, win.at[0], halo_send.at[0], halo_recv.at[0], next_chip),
        remote(rope_ref, win_r.at[0], halo_send.at[1], halo_recv.at[1], next_chip),
    ]
    give = 2 - 2 * core
    halo_mate = [
        remote(win.at[give], win.at[1], halo_send.at[2], halo_recv.at[2], mate),
        remote(win_r.at[give], win_r.at[1], halo_send.at[3], halo_recv.at[3], mate),
    ]
    flows = [(i, way) for i in range(3) for way in range(2)]

    def some(d):
        return [(i, way) for i, way in flows if d <= counts[way][i]]

    greet([{"ctx": lax.rem(me + d, n)} for d in (1, 2, 4, 6, n - 1, n - 2, n - 4, n - 6)])
    for d in (3, 2, 1):
        for i, way in flows:
            send(i, way, d).start()
    own = [pltpu.make_async_copy(srcs[i], bufs[i].at[me], own_sem.at[i]) for i in range(3)]
    own.append(pltpu.make_async_copy(lat_ref, win.at[2], own_sem.at[3]))
    own.append(pltpu.make_async_copy(rope_ref, win_r.at[2], own_sem.at[4]))
    for copy in own + halo:
        copy.start()
    for i in range(3):
        mate_copy(i, 0, 0, me).start()
    for i, way in flows:
        arrival(i, way, 3).wait_recv()
        for d in (6, 5, 4):
            send(i, way, d).start()
    for d in (1, 2):
        for i, way in flows:
            arrival(i, way, d).wait_recv()
    for i, way in flows:
        for d in (1, 2, 3):
            mate_copy(i, way, d, me).start()
    for i, way in flows:
        arrival(i, way, 6).wait_recv()
        for d in (8, 7):
            if d <= counts[way][i]:
                send(i, way, d).start()
    for copy in own:
        copy.wait()
    for copy in halo:
        copy.wait_recv()
    for copy in halo_mate:
        copy.start()
    for d in (4, 5):
        for i, way in flows:
            arrival(i, way, d).wait_recv()
    for i, way in flows:
        for d in (4, 5, 6):
            mate_copy(i, way, d, me).start()
    for d in (7, 8):
        for i, way in some(d):
            arrival(i, way, d).wait_recv()
            mate_copy(i, way, d, me).start()
    for i in range(3):
        mate_copy(i, 0, 0, me).wait_send()
        mate_copy(i, 0, 0, partner).wait_recv()
    for d in range(1, 9):
        for i, way in some(d):
            send(i, way, d).wait_send()
            mate_copy(i, way, d, me).wait_send()
            mate_copy(i, way, d, partner).wait_recv()
    for copy in halo:
        copy.wait_send()
    for copy in halo_mate:
        copy.wait_send()
        copy.wait_recv()


def gather(uk, uv, latent, rope, logp, base, docs, mask):
    sem = pltpu.SemaphoreType.DMA
    return pl.pallas_call(
        gather_kernel,
        out_shape=(
            jax.ShapeDtypeStruct((32,) + uk.shape, bf16),
            jax.ShapeDtypeStruct((32,) + uv.shape, bf16),
            jax.ShapeDtypeStruct((32, 8, 128), f32),
            jax.ShapeDtypeStruct((3,) + latent.shape, bf16),
            jax.ShapeDtypeStruct((3,) + rope.shape, bf16),
        ),
        in_specs=[VMEM] * 8,
        out_specs=(VMEM,) * 5,
        scratch_shapes=[
            pltpu.VMEM((8, 128), f32),
            sem((5,)), sem((3, 2, 9)), sem((3, 2, 9)), sem((3, 2, 9)), sem((3, 2, 9)), sem((4,)), sem((4,)),
        ],
        compiler_params=pltpu.CompilerParams(collective_id=0, has_side_effects=True),
    )(uk, uv, latent, rope, logp, base, docs, mask)


def dot_nt(a, b):
    return lax.dot_general(a, b, (((1,), (1,)), ((), ())), preferred_element_type=f32)


def dot_tn(a, b):
    return lax.dot_general(a, b, (((0,), (0,)), ((), ())), preferred_element_type=f32)


def dot_nn(a, b):
    return jnp.dot(a, b, preferred_element_type=f32)


def attend_kernel(
    win_ref, rope_ref, uk_ref, uv_ref, q_ref, qr_ref, og_ref, st_ref,
    dq_ref, dqr_ref, dwk_ref, dwv_ref, dl_ref, acc, lat_t, gscale, rope_k_ref, docs,
):
    step = pl.program_id(0)
    me = lax.axis_index("ctx")
    latent = win_ref[...]

    @pl.when(step == 0)
    def _():
        acc[...] = jnp.zeros_like(acc)
        lat_t[...] = latent.astype(f32).T.astype(bf16)
        sums = jnp.sum(jnp.sum(st_ref[...], axis=0), axis=1, keepdims=True)
        live_total, live_count = sums[0:1], sums[1:2]
        own = st_ref[me]
        gap = npo_beta * (live_total / live_count - own[3:4])
        weight = 2.0 * (1.0 / (1.0 + jnp.exp(-gap))) * 4096.0 / live_count
        gscale[...] = jnp.broadcast_to(weight * own[1:2], (128, 128)).T
        for t in range(3):
            rows = slice(t * 128, t * 128 + 128)
            there = st_ref[lax.rem(me + 30 + t, 32)]
            docs[rows, :] = jnp.broadcast_to(there[2:3], (128, 128)).T
            column = rope_ref[t].astype(f32).T
            rope_k_ref[rows, :] = jnp.concatenate([column, column], axis=1).astype(bf16)

    scale = 1.0 / math.sqrt(NOPE + ROPE)
    key_idx = lax.broadcasted_iota(jnp.int32, (384, 128), 0) - 256
    query_idx = lax.broadcasted_iota(jnp.int32, (384, 128), 1)
    allowed = docs[...] == st_ref[me][2:3]
    allowed = allowed & (key_idx <= query_idx) & (me * 128 + key_idx >= 0)
    low_lane = lax.broadcasted_iota(jnp.int32, (128, 128), 1) < ROPE
    keys = dot_nn(latent, uk_ref[...]).astype(bf16)
    values = dot_nn(latent, uv_ref[...]).astype(bf16)
    key_rope = rope_k_ref[...]
    query_rope = qr_ref[...].astype(f32)
    scale_col = gscale[...]
    part_k, part_v, rope_q, rope_k = [], [], [], 0.0
    for p in range(2):
        cols = slice(p * 128, p * 128 + 128)
        qn = q_ref[:, cols]
        mine = low_lane if p == 0 else jnp.logical_not(low_lane)
        qr = jnp.where(mine, query_rope, 0.0).astype(bf16)
        kh, vh = keys[:, cols], values[:, cols]
        grad = (scale_col * og_ref[:, cols].astype(f32)).astype(bf16)
        scores = dot_nt(kh, qn) + dot_nt(key_rope, qr)
        scores = jnp.where(allowed, scores * scale, -1e30)
        top = jnp.max(scores, axis=0, keepdims=True)
        expon = jnp.where(allowed, jnp.exp(scores - top), 0.0)
        probs = expon * (1.0 / jnp.sum(expon, axis=0, keepdims=True))
        low = probs.astype(bf16)
        dprob = dot_nt(vh, grad)
        delta = jnp.sum(low.astype(f32) * dprob, axis=0, keepdims=True)
        dscore = (probs * (dprob - delta) * scale).astype(bf16)
        dq_ref[:, cols] = dot_tn(dscore, kh).astype(bf16)
        rope_q.append(dot_tn(dscore, key_rope))
        rope_k = rope_k + dot_nn(dscore, qr)
        part_k.append(dot_nn(dscore, qn).astype(bf16))
        part_v.append(dot_nn(low, grad).astype(bf16))
    dqr_ref[...] = jnp.where(low_lane, rope_q[0], rope_q[1]).astype(bf16)
    part_k = jnp.concatenate(part_k, axis=1)
    part_v = jnp.concatenate(part_v, axis=1)
    acc[:, :512] += dot_nt(part_k, uk_ref[...]) + dot_nt(part_v, uv_ref[...])
    acc[:, 512:] += rope_k
    dwk_ref[...] = dot_nn(lat_t[...], part_k).astype(bf16)
    dwv_ref[...] = dot_nn(lat_t[...], part_v).astype(bf16)

    @pl.when(step == pl.num_programs(0) - 1)
    def _():
        for t in range(3):
            dl_ref[:, t] = acc[t * 128:t * 128 + 128, :].reshape(16, 8, 640).astype(bf16)


def attend(window, rope, uk, uv, q_nope, q_rope, out_grad, stats):
    width = uk.shape[1]

    def cols(rows, block):
        return pl.BlockSpec((rows, block), lambda i: (0, i))

    def whole(shape):
        return pl.BlockSpec(shape, lambda i: (0,) * len(shape))

    return pl.pallas_call(
        attend_kernel,
        grid=(width // 256,),
        out_shape=(
            jax.ShapeDtypeStruct(q_nope.shape, bf16),
            jax.ShapeDtypeStruct(q_rope.shape, bf16),
            jax.ShapeDtypeStruct((512, width), bf16),
            jax.ShapeDtypeStruct((512, width), bf16),
            jax.ShapeDtypeStruct((16, 3, 8, 640), bf16),
        ),
        in_specs=[
            whole((384, 512)), whole((3, 64, 128)), cols(512, 256), cols(512, 256), cols(128, 256),
            cols(128, 128), cols(128, 256), whole(stats.shape),
        ],
        out_specs=(cols(128, 256), cols(128, 128), cols(512, 256), cols(512, 256), whole((16, 3, 8, 640))),
        scratch_shapes=[
            pltpu.VMEM((384, 640), f32), pltpu.VMEM((512, 384), bf16), pltpu.VMEM((128, 128), f32),
            pltpu.VMEM((384, 128), bf16), pltpu.VMEM((384, 128), f32),
        ],
        compiler_params=pltpu.CompilerParams(dimension_semantics=("arbitrary",)),
    )(window, rope, uk, uv, q_nope, q_rope, out_grad, stats)


def reduce_kernel(
    dwk, dwv, dl, ok, ov, final, par_buf, recv_buf, send_buf, inbox, halves, back, mine,
    par_send, par_recv, ring_send, ring_recv, back_send, back_recv, mix_send, mix_recv, all_send, all_recv,
):
    me, col = lax.axis_index("ctx"), lax.axis_index("dp")
    n, m = 32, 16
    core = lax.rem(me, 2)
    partner = me + 1 - 2 * core
    mate = {"ctx": partner}
    grads, counts = (dwk, dwv), ((8, 7), (7, 8))
    others = [lax.rem(col + k, m) for k in range(1, m)]
    flows = [(i, way) for i in range(2) for way in range(2)]

    def away(way, hops):
        return lax.rem(me + 2 * hops, n) if way == 0 else lax.rem(me + n - 2 * hops, n)

    def to_mate(i, d):
        src = grads[i].at[lax.rem(partner + 2 * d, n)]
        return remote(src, par_buf.at[i, d], par_send.at[i, d], par_recv.at[i, d], mate)

    def mix_copy(k):
        return remote(
            dl.at[others[k - 1]], inbox.at[k - 1], mix_send.at[k - 1], mix_recv.at[k - 1],
            {"dp": others[k - 1]},
        )

    def back_copy(d):
        peer = {"ctx": lax.rem(me + n - d, n)}
        return remote(halves.at[d - 1], back.at[d - 1], back_send.at[d - 1], back_recv.at[d - 1], peer)

    def all_copy(k):
        return remote(mine, final.at[k], all_send.at[k - 1], all_recv.at[k - 1], {"dp": others[k - 1]})

    def ring(i, way, d):
        peer = {"ctx": away(way, d - relay(d))}
        return remote(
            send_buf.at[i, way, d], recv_buf.at[i, way, d], ring_send.at[i, way, d],
            ring_recv.at[i, way, d], peer,
        )

    def local(i, d):
        to_mate(i, d).wait_recv()
        total = grads[i][lax.rem(me + 2 * d, n)].astype(f32)
        return total + par_buf[i, d].astype(f32)

    def arrived(i, way, first, last):
        total = 0.0
        for d in range(first, min(last, counts[way][i]) + 1):
            ring(i, way, d).wait_recv()
            total = total + recv_buf[i, way, d].astype(f32)
        return total

    def pass_on(i, way, d):
        total = local(i, d if way == 0 else 16 - d)
        if d in (3, 6):
            total = total + arrived(i, way, d + 1, d + 3)
        send_buf[i, way, d] = total.astype(bf16)
        ring(i, way, d).start()

    greet(
        [{"ctx": lax.rem(me + d, n)} for d in (1, 2, 4, 6, n - 1, n - 2, n - 4, n - 6)]
        + [{"dp": k} for k in others]
    )
    order = (8, 7, 9, 5, 11, 4, 12, 2, 14, 1, 15, 6, 10, 3, 13, 0)
    for d in order[:3]:
        for i in range(2):
            to_mate(i, d).start()
    for k in range(1, m):
        mix_copy(k).start()
    for d in order[3:]:
        for i in range(2):
            to_mate(i, d).start()
    for d in (8, 7, 5, 4):
        for i, way in flows:
            if d <= counts[way][i]:
                pass_on(i, way, d)
    for i, way in flows:
        pass_on(i, way, 6)
    total = dl[col].astype(f32)
    for k in range(1, m):
        mix_copy(k).wait_recv()
        total = total + inbox[k - 1].astype(f32)
    halves[0] = total[1].astype(bf16)
    halves[1] = total[0].astype(bf16)
    for d in (2, 1):
        back_copy(d).start()
    for d in (2, 1):
        for i, way in flows:
            pass_on(i, way, d)
    for i, way in flows:
        pass_on(i, way, 3)
    total = total[2]
    for d in (2, 1):
        back_copy(d).wait_recv()
        total = total + back[d - 1].astype(f32)
    rope = total[:, 512:]
    rope = rope + pltpu.roll(rope, 64, 1)
    rows = jnp.concatenate([total[:, :512], rope], axis=1).astype(bf16)
    mine[...] = rows
    final[0] = rows
    for k in range(1, m):
        all_copy(k).start()
    outs = (ok, ov)
    for i in range(2):
        outs[i][...] = local(i, 0) + arrived(i, 0, 1, 3) + arrived(i, 1, 1, 3)
    for k in range(1, m):
        all_copy(k).wait_recv()
    for i in range(2):
        for d in range(16):
            to_mate(i, d).wait_send()
        for way in range(2):
            for d in range(1, counts[way][i] + 1):
                ring(i, way, d).wait_send()
    for d in (2, 1):
        back_copy(d).wait_send()
    for k in range(1, m):
        mix_copy(k).wait_send()
        all_copy(k).wait_send()


def reduce(dwk, dwv, dl):
    sem = pltpu.SemaphoreType.DMA
    width = dwk.shape[2]
    return pl.pallas_call(
        reduce_kernel,
        out_shape=(
            jax.ShapeDtypeStruct((16, width), f32),
            jax.ShapeDtypeStruct((16, width), f32),
            jax.ShapeDtypeStruct((16, 8, 640), bf16),
        ),
        in_specs=[VMEM] * 3,
        out_specs=(VMEM,) * 3,
        scratch_shapes=[
            pltpu.VMEM((2, 16, 16, width), bf16),
            pltpu.VMEM((2, 2, 9, 16, width), bf16),
            pltpu.VMEM((2, 2, 9, 16, width), bf16),
            pltpu.VMEM((15, 3, 8, 640), bf16),
            pltpu.VMEM((2, 8, 640), bf16),
            pltpu.VMEM((2, 8, 640), bf16),
            pltpu.VMEM((8, 640), bf16),
            sem((2, 16)), sem((2, 16)), sem((2, 2, 9)), sem((2, 2, 9)),
            sem((2,)), sem((2,)), sem((15,)), sem((15,)), sem((15,)), sem((15,)),
        ],
        compiler_params=pltpu.CompilerParams(collective_id=1, has_side_effects=True),
    )(dwk, dwv, dl)


def place_kernel(wk_ref, wv_ref, rows_ref, ok, ov, olat, orope):
    col = lax.axis_index("dp")
    ok[...] = wk_ref[...]
    ov[...] = wv_ref[...]
    pieces = [rows_ref[lax.rem(col + 16 - j, 16)].astype(f32) for j in range(16)]
    rows = jnp.concatenate(pieces, axis=0)
    olat[...] = rows[:, :512].astype(bf16)
    orope[...] = rows[:, 512:].T[:ROPE].astype(bf16)


def place(wk, wv, rows):
    return pl.pallas_call(
        place_kernel,
        out_shape=(
            jax.ShapeDtypeStruct(wk.shape, f32),
            jax.ShapeDtypeStruct(wv.shape, f32),
            jax.ShapeDtypeStruct((128, 512), bf16),
            jax.ShapeDtypeStruct((ROPE, 128), bf16),
        ),
        in_specs=[VMEM] * 3,
        out_specs=(VMEM,) * 4,
    )(wk, wv, rows)


def on_device(
    q_nope, q_rope, latent, k_rope, w_uk, w_uv, out_grad, log_prob, ref_logp, doc_ids, loss_mask
):
    full_uk, full_uv, stats, window, rope = gather(
        w_uk, w_uv, latent, k_rope.T, log_prob[None, :], ref_logp[None, :], doc_ids[None, :],
        loss_mask[None, :],
    )
    width = w_uk.shape[1]
    dq_nope, dq_rope, dwk, dwv, dl = attend(
        window.reshape(384, 512), rope, full_uk.reshape(512, width),
        full_uv.reshape(512, width), q_nope, q_rope, out_grad, stats,
    )
    dw_uk, dw_uv, d_latent, d_krope = place(
        *reduce(dwk.reshape(32, 16, width), dwv.reshape(32, 16, width), dl)
    )
    return dq_nope, dq_rope, d_latent, d_krope.T, dw_uk, dw_uv


def solution(mesh):
    both, rows, flat = P("ctx", "dp"), P("ctx", None), P("ctx")
    return jax.shard_map(
        on_device,
        mesh=mesh,
        in_specs=(both, both, rows, rows, both, both, both, flat, P(), flat, flat),
        out_specs=(both, both, rows, rows, both, both),
        check_vma=False,
    )
```

time: 111 us -> 94.9 us (0.85)
  the two profiles are of different devices: /device:TPU:2 before, /device:TPU:1 now
where the time goes in v2:
time: 94.9 us; the launch traced here: 94.6 us
  Pallas kernels  93.3 us (98%)
  between operations  1.3 us (1%)
    pallas_call x1, Pallas kernels, gather(): pl.pallas_call(gather_kernel, out_shape=(jax.ShapeDtypeStruct((32,) + uk....  45.8 us
    pallas_call x1, Pallas kernels, reduce(): pl.pallas_call(reduce_kernel, out_shape=(jax.ShapeDtypeStruct((16, width)...  34.2 us
    pallas_call x1, Pallas kernels, attend(): pl.pallas_call(attend_kernel, grid=(width // 256,), out_shape=(jax.ShapeD...  11.6 us

profile of v2, /device:TPU:1, one launch (start us, length us, event | category | flops | bytes accessed | tf_op | source)
XLA Modules:
  0.0 94.6 jit_solution(7110876796654422407)
XLA Ops:
  1.3 45.8 %shard_map.154 = (bf16[32,16,1024]{2,1,0:T(8,128)(2,1)}, bf16[32,16,1024]{2,1,0:T(8,128)(2,1)}, f32[32,8,128]{2,1,0:T(8,128)}, bf16[3,128,512]{2,1,0:T(8,128)(2,1)}, bf16[3,64,128]{2,1,0:T(8,128)(2,1)}) custom-call(bf16[16,1024]{1,0:T(8,128)(2,1)} %uk_ref.1, bf16[16,1024]{1,0:T(8,128)(2,1)} %uv_ref.1, bf16[128,512]{1,0:T(8,128)(2,1)} %lat_ref.1, ...), custom_call_target="tpu_custom_call" | custom-call | tf_op jit(solution)/shard_map/pallas_call | solution.py:152
  47.1 11.6 %shard_map.155 = (bf16[128,1024]{1,0:T(8,128)(2,1)}, bf16[128,512]{1,0:T(8,128)(2,1)}, bf16[512,1024]{1,0:T(8,128)(2,1)}, bf16[512,1024]{1,0:T(8,128)(2,1)}, bf16[16,3,8,640]{3,2,1,0:T(8,128)(2,1)}) custom-call(bf16[384,512]{1,0:T(8,128)(2,1)} %bitcast.16, bf16[3,64,128]{2,1,0:T(8,128)(2,1)} %get-tuple-element.24.rope_ref, bf16[512,1024]{1,0:T(8,128)(2,1)} %bitcast.12, ...), custom_call_target="tpu_custom_call" | custom-call | tf_op jit(solution)/shard_map/pallas_call | solution.py:264
  58.7 34.2 %shard_map.156 = (f32[16,1024]{1,0:T(8,128)}, f32[16,1024]{1,0:T(8,128)}, bf16[16,8,640]{2,1,0:T(8,128)(2,1)}) custom-call(bf16[32,16,1024]{2,1,0:T(8,128)(2,1)} %bitcast.14, bf16[32,16,1024]{2,1,0:T(8,128)(2,1)} %bitcast.15, bf16[16,3,8,640]{3,2,1,0:T(8,128)(2,1)} %get-tuple-element.32.dl), custom_call_target="tpu_custom_call" | custom-call | tf_op jit(solution)/shard_map/pallas_call | solution.py:410
  92.9 1.7 %shard_map.157 = (f32[16,1024]{1,0:T(8,128)}, f32[16,1024]{1,0:T(8,128)}, bf16[128,512]{1,0:T(8,128)(2,1)}, bf16[64,128]{1,0:T(8,128)(2,1)}) custom-call(f32[16,1024]{1,0:T(8,128)} %get-tuple-element.33.wk_ref, f32[16,1024]{1,0:T(8,128)} %get-tuple-element.34.wv_ref, bf16[16,8,640]{2,1,0:T(8,128)(2,1)} %get-tuple-element.35.rows_ref), custom_call_target="tpu_custom_call" | custom-call | tf_op jit(solution)/shard_map/pallas_call | solution.py:445

commit v3 on v2

v3 whole, which is shorter than its diff:
```python
import math

import jax
import jax.numpy as jnp
from jax import lax
from jax.experimental import pallas as pl
from jax.experimental.pallas import tpu as pltpu
from jax.sharding import PartitionSpec as P

NOPE = 128
ROPE = 64
npo_beta = 1.0
MESH = pl.DeviceIdType.MESH
VMEM = pl.BlockSpec(memory_space=pltpu.VMEM)
f32 = jnp.float32
bf16 = jnp.bfloat16


def greet(peers):
    barrier = pltpu.get_barrier_semaphore()
    for peer in peers:
        pl.semaphore_signal(barrier, inc=1, device_id=peer, device_id_type=MESH)
    pl.semaphore_wait(barrier, len(peers))


def remote(src, dst, send, recv, peer):
    return pltpu.make_async_remote_copy(
        src_ref=src, dst_ref=dst, send_sem=send, recv_sem=recv, device_id=peer, device_id_type=MESH
    )


def relay(d):
    return 3 * ((d - 1) // 3)


def gather_kernel(
    uk_ref, uv_ref, lat_ref, rope_ref, logp_ref, doc_ref, mask_ref,
    buf, win, item, near,
    own_sem, ring_send, ring_recv, par_send, par_recv, halo_send, halo_recv,
):
    me = lax.axis_index("ctx")
    n = 32
    core = lax.rem(me, 2)
    partner = me + 1 - 2 * core
    mate = {"ctx": partner}
    counts = (7, 8)
    width = uk_ref.shape[1]

    item[:, :width] = uk_ref[...]
    item[:, width:2 * width] = uv_ref[...]
    mask = mask_ref[...].astype(f32)
    masked = mask * logp_ref[...]
    high = masked.astype(bf16).astype(f32)
    rest = masked - high
    middle = rest.astype(bf16).astype(f32)
    small = [doc_ref[...].astype(f32), mask, high, middle, rest - middle, jnp.zeros((11, 128), f32)]
    item[:, 2 * width:] = jnp.concatenate(small, axis=0).astype(bf16)
    near[:, :512] = lat_ref[...]
    column = rope_ref[...].astype(f32).T
    near[:, 512:] = jnp.concatenate([column, column], axis=1).astype(bf16)

    def away(way, hops):
        return lax.rem(me + 2 * hops, n) if way == 0 else lax.rem(me + n - 2 * hops, n)

    def origin(base, way, d):
        return lax.rem(base + n - 2 * d, n) if way == 0 else lax.rem(base + 2 * d, n)

    def send(way, d):
        slot = buf.at[origin(me, way, relay(d))]
        src = item if relay(d) == 0 else slot
        peer = {"ctx": away(way, d - relay(d))}
        return remote(src, slot, ring_send.at[way, d], ring_recv.at[way, d], peer)

    def arrival(way, d):
        slot = buf.at[origin(me, way, d)]
        peer = {"ctx": away(1 - way, d - relay(d))}
        return remote(slot, slot, ring_send.at[way, d], ring_recv.at[way, d], peer)

    def mate_copy(way, d, base):
        slot = buf.at[origin(base, way, d)]
        src = item if d == 0 else slot
        return remote(src, slot, par_send.at[way, d], par_recv.at[way, d], mate)

    halo = remote(near, win.at[0], halo_send.at[0], halo_recv.at[0], {"ctx": away(0, 1)})
    halo_mate = remote(win.at[2 - 2 * core], win.at[1], halo_send.at[1], halo_recv.at[1], mate)
    ways = (1, 0)

    greet([{"ctx": lax.rem(me + d, n)} for d in (1, 2, 4, 6, n - 1, n - 2, n - 4, n - 6)])
    for d in (3, 2, 1):
        for way in ways:
            send(way, d).start()
    own = [
        pltpu.make_async_copy(item, buf.at[me], own_sem.at[0]),
        pltpu.make_async_copy(near, win.at[2], own_sem.at[1]),
    ]
    for copy in own:
        copy.start()
    mate_copy(0, 0, me).start()
    halo.start()
    for way in ways:
        arrival(way, 3).wait_recv()
        for d in (6, 5, 4):
            send(way, d).start()
    for d in (1, 2):
        for way in ways:
            arrival(way, d).wait_recv()
    for d in (1, 2, 3):
        for way in ways:
            mate_copy(way, d, me).start()
    for way in ways:
        arrival(way, 6).wait_recv()
        for d in (8, 7):
            if d <= counts[way]:
                send(way, d).start()
    for copy in own:
        copy.wait()
    halo.wait_recv()
    halo_mate.start()
    for d in (4, 5):
        for way in ways:
            arrival(way, d).wait_recv()
    for d in (4, 5, 6):
        for way in ways:
            mate_copy(way, d, me).start()
    for d in (7, 8):
        for way in ways:
            if d <= counts[way]:
                arrival(way, d).wait_recv()
                mate_copy(way, d, me).start()
    mate_copy(0, 0, me).wait_send()
    mate_copy(0, 0, partner).wait_recv()
    for d in range(1, 9):
        for way in ways:
            if d <= counts[way]:
                send(way, d).wait_send()
                mate_copy(way, d, me).wait_send()
                mate_copy(way, d, partner).wait_recv()
    halo.wait_send()
    halo_mate.wait_send()
    halo_mate.wait_recv()


def gather(uk, uv, latent, rope, logp, docs, mask):
    sem = pltpu.SemaphoreType.DMA
    total = 2 * uk.shape[1] + 128
    return pl.pallas_call(
        gather_kernel,
        out_shape=(
            jax.ShapeDtypeStruct((32, 16, total), bf16),
            jax.ShapeDtypeStruct((3, 128, 640), bf16),
        ),
        in_specs=[VMEM] * 7,
        out_specs=(VMEM,) * 2,
        scratch_shapes=[
            pltpu.VMEM((16, total), bf16),
            pltpu.VMEM((128, 640), bf16),
            sem((2,)), sem((2, 9)), sem((2, 9)), sem((2, 9)), sem((2, 9)), sem((2,)), sem((2,)),
        ],
        compiler_params=pltpu.CompilerParams(collective_id=0, has_side_effects=True),
    )(uk, uv, latent, rope, logp, docs, mask)


def dot_nt(a, b):
    return lax.dot_general(a, b, (((1,), (1,)), ((), ())), preferred_element_type=f32)


def dot_tn(a, b):
    return lax.dot_general(a, b, (((0,), (0,)), ((), ())), preferred_element_type=f32)


def dot_nn(a, b):
    return jnp.dot(a, b, preferred_element_type=f32)


def small_rows(st_ref, idx):
    return st_ref[pl.ds(pl.multiple_of(idx * 16, 16), 16), :].astype(f32)


def attend_kernel(
    win_ref, uk_ref, uv_ref, q_ref, qr_ref, og_ref, st_ref, base_ref,
    dq_ref, dqr_ref, dw_ref, dl_ref, acc, lat_t, gscale, docs,
):
    step = pl.program_id(0)
    me = lax.axis_index("ctx")
    latent = win_ref[:, :512]

    @pl.when(step == 0)
    def _():
        acc[...] = jnp.zeros_like(acc)
        lat_t[...] = latent.astype(f32).T.astype(bf16)
        every = st_ref[...].astype(f32).reshape(32, 16, 128)
        sums = jnp.sum(jnp.sum(every, axis=0), axis=1, keepdims=True)
        live_count, live_total = sums[1:2], sums[2:3] + sums[3:4] + sums[4:5]
        own = small_rows(st_ref, me)
        gap = npo_beta * (live_total / live_count - base_ref[...])
        weight = 2.0 * (1.0 / (1.0 + jnp.exp(-gap))) * 4096.0 / live_count
        gscale[...] = jnp.broadcast_to(weight * own[1:2], (128, 128)).T
        for t in range(3):
            there = small_rows(st_ref, lax.rem(me + 30 + t, 32))
            docs[t * 128:t * 128 + 128, :] = jnp.broadcast_to(there[0:1], (128, 128)).T

    scale = 1.0 / math.sqrt(NOPE + ROPE)
    key_idx = lax.broadcasted_iota(jnp.int32, (384, 128), 0) - 256
    query_idx = lax.broadcasted_iota(jnp.int32, (384, 128), 1)
    allowed = docs[...] == small_rows(st_ref, me)[0:1]
    allowed = allowed & (key_idx <= query_idx) & (me * 128 + key_idx >= 0)
    low_lane = lax.broadcasted_iota(jnp.int32, (128, 128), 1) < ROPE
    keys = dot_nn(latent, uk_ref[...]).astype(bf16)
    values = dot_nn(latent, uv_ref[...]).astype(bf16)
    key_rope = win_ref[:, 512:]
    query_rope = qr_ref[...].astype(f32)
    scale_col = gscale[...]
    part_k, part_v, rope_q, rope_k = [], [], [], 0.0
    for p in range(2):
        cols = slice(p * 128, p * 128 + 128)
        qn = q_ref[:, cols]
        mine = low_lane if p == 0 else jnp.logical_not(low_lane)
        qr = jnp.where(mine, query_rope, 0.0).astype(bf16)
        kh, vh = keys[:, cols], values[:, cols]
        grad = (scale_col * og_ref[:, cols].astype(f32)).astype(bf16)
        scores = dot_nt(kh, qn) + dot_nt(key_rope, qr)
        scores = jnp.where(allowed, scores * scale, -1e30)
        top = jnp.max(scores, axis=0, keepdims=True)
        expon = jnp.where(allowed, jnp.exp(scores - top), 0.0)
        probs = expon * (1.0 / jnp.sum(expon, axis=0, keepdims=True))
        low = probs.astype(bf16)
        dprob = dot_nt(vh, grad)
        delta = jnp.sum(low.astype(f32) * dprob, axis=0, keepdims=True)
        dscore = (probs * (dprob - delta) * scale).astype(bf16)
        dq_ref[:, cols] = dot_tn(dscore, kh).astype(bf16)
        rope_q.append(dot_tn(dscore, key_rope))
        rope_k = rope_k + dot_nn(dscore, qr)
        part_k.append(dot_nn(dscore, qn).astype(bf16))
        part_v.append(dot_nn(low, grad).astype(bf16))
    dqr_ref[...] = jnp.where(low_lane, rope_q[0], rope_q[1]).astype(bf16)
    part_k = jnp.concatenate(part_k, axis=1)
    part_v = jnp.concatenate(part_v, axis=1)
    acc[:, :512] += dot_nt(part_k, uk_ref[...]) + dot_nt(part_v, uv_ref[...])
    acc[:, 512:] += rope_k
    half = pl.num_programs(0) * 256
    first = pl.multiple_of(step * 256, 256)
    dw_ref[:, pl.ds(first, 256)] = dot_nn(lat_t[...], part_k).astype(bf16)
    dw_ref[:, pl.ds(pl.multiple_of(half + first, 256), 256)] = dot_nn(lat_t[...], part_v).astype(bf16)

    @pl.when(step == pl.num_programs(0) - 1)
    def _():
        for t in range(3):
            dl_ref[:, t] = acc[t * 128:t * 128 + 128, :].reshape(16, 8, 640).astype(bf16)


def attend(window, full, q_nope, q_rope, out_grad, base):
    width = q_nope.shape[1]

    def cols(rows, block):
        return pl.BlockSpec((rows, block), lambda i: (0, i))

    def whole(shape):
        return pl.BlockSpec(shape, lambda i: (0,) * len(shape))

    return pl.pallas_call(
        attend_kernel,
        grid=(width // 256,),
        out_shape=(
            jax.ShapeDtypeStruct(q_nope.shape, bf16),
            jax.ShapeDtypeStruct(q_rope.shape, bf16),
            jax.ShapeDtypeStruct((512, 2 * width), bf16),
            jax.ShapeDtypeStruct((16, 3, 8, 640), bf16),
        ),
        in_specs=[
            whole((384, 640)), cols(512, 256), pl.BlockSpec((512, 256), lambda i: (0, i + width // 256)),
            cols(128, 256), cols(128, 128), cols(128, 256),
            pl.BlockSpec((512, 128), lambda i: (0, width // 64)), whole((1, 1)),
        ],
        out_specs=(cols(128, 256), cols(128, 128), whole((512, 2 * width)), whole((16, 3, 8, 640))),
        scratch_shapes=[
            pltpu.VMEM((384, 640), f32), pltpu.VMEM((512, 384), bf16), pltpu.VMEM((128, 128), f32),
            pltpu.VMEM((384, 128), f32),
        ],
        compiler_params=pltpu.CompilerParams(dimension_semantics=("arbitrary",)),
    )(window, full, full, q_nope, q_rope, out_grad, full, base)


def reduce_kernel(
    dw, dl, ok, ov, final, par_buf, recv_buf, send_buf, inbox, halves, back, mine,
    par_send, par_recv, ring_send, ring_recv, back_send, back_recv, mix_send, mix_recv, all_send, all_recv,
):
    me, col = lax.axis_index("ctx"), lax.axis_index("dp")
    n, m = 32, 16
    core = lax.rem(me, 2)
    partner = me + 1 - 2 * core
    mate = {"ctx": partner}
    counts = (8, 7)
    others = [lax.rem(col + k, m) for k in range(1, m)]
    width = ok.shape[1]

    def away(way, hops):
        return lax.rem(me + 2 * hops, n) if way == 0 else lax.rem(me + n - 2 * hops, n)

    def to_mate(d):
        src = dw.at[lax.rem(partner + 2 * d, n)]
        return remote(src, par_buf.at[d], par_send.at[d], par_recv.at[d], mate)

    def mix_copy(k):
        return remote(
            dl.at[others[k - 1]], inbox.at[k - 1], mix_send.at[k - 1], mix_recv.at[k - 1],
            {"dp": others[k - 1]},
        )

    def back_copy(d):
        peer = {"ctx": lax.rem(me + n - d, n)}
        return remote(halves.at[d - 1], back.at[d - 1], back_send.at[d - 1], back_recv.at[d - 1], peer)

    def all_copy(k):
        return remote(mine, final.at[k], all_send.at[k - 1], all_recv.at[k - 1], {"dp": others[k - 1]})

    def ring(way, d):
        peer = {"ctx": away(way, d - relay(d))}
        return remote(
            send_buf.at[way, d], recv_buf.at[way, d], ring_send.at[way, d], ring_recv.at[way, d], peer
        )

    def local(d):
        to_mate(d).wait_recv()
        return dw[lax.rem(me + 2 * d, n)].astype(f32) + par_buf[d].astype(f32)

    def arrived(way, first, last):
        total = 0.0
        for d in range(first, min(last, counts[way]) + 1):
            ring(way, d).wait_recv()
            total = total + recv_buf[way, d].astype(f32)
        return total

    def pass_on(way, d):
        total = local(d if way == 0 else 16 - d)
        if d in (3, 6):
            total = total + arrived(way, d + 1, d + 3)
        send_buf[way, d] = total.astype(bf16)
        ring(way, d).start()

    greet(
        [{"ctx": lax.rem(me + d, n)} for d in (1, 2, 4, 6, n - 1, n - 2, n - 4, n - 6)]
        + [{"dp": k} for k in others]
    )
    order = (8, 7, 9, 5, 11, 4, 12, 2, 14, 1, 15, 6, 10, 3, 13, 0)
    for d in order[:3]:
        to_mate(d).start()
    for k in range(1, m):
        mix_copy(k).start()
    for d in order[3:]:
        to_mate(d).start()
    for d in (8, 7, 5, 4):
        for way in range(2):
            if d <= counts[way]:
                pass_on(way, d)
    for way in range(2):
        pass_on(way, 6)
    total = dl[col].astype(f32)
    for k in range(1, m):
        mix_copy(k).wait_recv()
        total = total + inbox[k - 1].astype(f32)
    halves[0] = total[1].astype(bf16)
    halves[1] = total[0].astype(bf16)
    for d in (2, 1):
        back_copy(d).start()
    for d in (2, 1, 3):
        for way in range(2):
            pass_on(way, d)
    total = total[2]
    for d in (2, 1):
        back_copy(d).wait_recv()
        total = total + back[d - 1].astype(f32)
    rope = total[:, 512:]
    rope = rope + pltpu.roll(rope, 64, 1)
    rows = jnp.concatenate([total[:, :512], rope], axis=1).astype(bf16)
    mine[...] = rows
    final[0] = rows
    for k in range(1, m):
        all_copy(k).start()
    total = local(0) + arrived(0, 1, 3) + arrived(1, 1, 3)
    ok[...] = total[:, :width]
    ov[...] = total[:, width:]
    for k in range(1, m):
        all_copy(k).wait_recv()
    for d in range(16):
        to_mate(d).wait_send()
    for way in range(2):
        for d in range(1, counts[way] + 1):
            ring(way, d).wait_send()
    for d in (2, 1):
        back_copy(d).wait_send()
    for k in range(1, m):
        mix_copy(k).wait_send()
        all_copy(k).wait_send()


def reduce(dw, dl):
    sem = pltpu.SemaphoreType.DMA
    width = dw.shape[2] // 2
    return pl.pallas_call(
        reduce_kernel,
        out_shape=(
            jax.ShapeDtypeStruct((16, width), f32),
            jax.ShapeDtypeStruct((16, width), f32),
            jax.ShapeDtypeStruct((16, 8, 640), bf16),
        ),
        in_specs=[VMEM] * 2,
        out_specs=(VMEM,) * 3,
        scratch_shapes=[
            pltpu.VMEM((16, 16, 2 * width), bf16),
            pltpu.VMEM((2, 9, 16, 2 * width), bf16),
            pltpu.VMEM((2, 9, 16, 2 * width), bf16),
            pltpu.VMEM((15, 3, 8, 640), bf16),
            pltpu.VMEM((2, 8, 640), bf16),
            pltpu.VMEM((2, 8, 640), bf16),
            pltpu.VMEM((8, 640), bf16),
            sem((16,)), sem((16,)), sem((2, 9)), sem((2, 9)),
            sem((2,)), sem((2,)), sem((15,)), sem((15,)), sem((15,)), sem((15,)),
        ],
        compiler_params=pltpu.CompilerParams(collective_id=1, has_side_effects=True),
    )(dw, dl)


def place_kernel(wk_ref, wv_ref, rows_ref, ok, ov, olat, orope):
    col = lax.axis_index("dp")
    ok[...] = wk_ref[...]
    ov[...] = wv_ref[...]
    pieces = [rows_ref[lax.rem(col + 16 - j, 16)].astype(f32) for j in range(16)]
    rows = jnp.concatenate(pieces, axis=0)
    olat[...] = rows[:, :512].astype(bf16)
    orope[...] = rows[:, 512:].T[:ROPE].astype(bf16)


def place(wk, wv, rows):
    return pl.pallas_call(
        place_kernel,
        out_shape=(
            jax.ShapeDtypeStruct(wk.shape, f32),
            jax.ShapeDtypeStruct(wv.shape, f32),
            jax.ShapeDtypeStruct((128, 512), bf16),
            jax.ShapeDtypeStruct((ROPE, 128), bf16),
        ),
        in_specs=[VMEM] * 3,
        out_specs=(VMEM,) * 4,
    )(wk, wv, rows)


def on_device(
    q_nope, q_rope, latent, k_rope, w_uk, w_uv, out_grad, log_prob, ref_logp, doc_ids, loss_mask
):
    full, window = gather(
        w_uk, w_uv, latent, k_rope.T, log_prob[None, :], doc_ids[None, :], loss_mask[None, :]
    )
    width = w_uk.shape[1]
    dq_nope, dq_rope, dw, dl = attend(
        window.reshape(384, 640), full.reshape(512, 2 * width + 128), q_nope, q_rope, out_grad,
        ref_logp[None, :],
    )
    dw_uk, dw_uv, d_latent, d_krope = place(*reduce(dw.reshape(32, 16, 2 * width), dl))
    return dq_nope, dq_rope, d_latent, d_krope.T, dw_uk, dw_uv


def solution(mesh):
    both, rows, flat = P("ctx", "dp"), P("ctx", None), P("ctx")
    return jax.shard_map(
        on_device,
        mesh=mesh,
        in_specs=(both, both, rows, rows, both, both, both, flat, P(), flat, flat),
        out_specs=(both, both, rows, rows, both, both),
        check_vma=False,
    )
```

time: 94.9 us -> 91.2 us (0.961)
  Pallas kernels: 93.3 us -> 89.6 us
    pallas_call x1, Pallas kernels: 45.8 us -> 41.8 us  [gather(): pl.pallas_call(gather_kernel, out_shape=(jax.ShapeDtypeStruct((32, 16, to...]
where the time goes in v3:
time: 91.2 us; the launch traced here: 90.9 us
  Pallas kernels  89.6 us (98%)
  between operations  1.3 us (1%)
    pallas_call x1, Pallas kernels, gather(): pl.pallas_call(gather_kernel, out_shape=(jax.ShapeDtypeStruct((32, 16, to...  41.8 us
    pallas_call x1, Pallas kernels, reduce(): pl.pallas_call(reduce_kernel, out_shape=(jax.ShapeDtypeStruct((16, width)...  34 us
    pallas_call x1, Pallas kernels, attend(): pl.pallas_call(attend_kernel, grid=(width // 256,), out_shape=(jax.ShapeD...  12.1 us

profile of v3, /device:TPU:1, one launch (start us, length us, event | category | flops | bytes accessed | tf_op | source)
XLA Modules:
  0.0 90.9 jit_solution(4992592402181107134)
XLA Ops:
  1.3 41.8 %shard_map.154 = (bf16[32,16,2176]{2,1,0:T(8,128)(2,1)}, bf16[3,128,640]{2,1,0:T(8,128)(2,1)}) custom-call(bf16[16,1024]{1,0:T(8,128)(2,1)} %uk_ref.1, bf16[16,1024]{1,0:T(8,128)(2,1)} %uv_ref.1, bf16[128,512]{1,0:T(8,128)(2,1)} %lat_ref.1, bf16[64,128]{1,0:T(8,128)(2,1)} %bitcast.15, f32[1,128]{1,0:T(1,128)} %bitcast.16, s32[1,128]{1,0:T(1,128)} %bitcast.17, ...), custom_call_target="tpu_custom_call" | custom-call | tf_op jit(solution)/shard_map/pallas_call | solution.py:146
  43.1 12.1 %shard_map.155 = (bf16[128,1024]{1,0:T(8,128)(2,1)}, bf16[128,512]{1,0:T(8,128)(2,1)}, bf16[512,2048]{1,0:T(8,128)(2,1)}, bf16[16,3,8,640]{3,2,1,0:T(8,128)(2,1)}) custom-call(bf16[384,640]{1,0:T(8,128)(2,1)} %bitcast.14, bf16[512,2176]{1,0:T(8,128)(2,1)} %bitcast.10, bf16[512,2176]{1,0:T(8,128)(2,1)} %bitcast.11, bf16[128,1024]{1,0:T(8,128)(2,1)} %q_ref.1, ...), custom_call_target="tpu_custom_call" | custom-call | tf_op jit(solution)/shard_map/pallas_call | solution.py:260
  55.2 34.0 %shard_map.156 = (f32[16,1024]{1,0:T(8,128)}, f32[16,1024]{1,0:T(8,128)}, bf16[16,8,640]{2,1,0:T(8,128)(2,1)}) custom-call(bf16[32,16,2048]{2,1,0:T(8,128)(2,1)} %bitcast.13, bf16[16,3,8,640]{3,2,1,0:T(8,128)(2,1)} %get-tuple-element.24.dl), custom_call_target="tpu_custom_call" | custom-call | tf_op jit(solution)/shard_map/pallas_call | solution.py:399
  89.2 1.7 %shard_map.157 = (f32[16,1024]{1,0:T(8,128)}, f32[16,1024]{1,0:T(8,128)}, bf16[128,512]{1,0:T(8,128)(2,1)}, bf16[64,128]{1,0:T(8,128)(2,1)}) custom-call(f32[16,1024]{1,0:T(8,128)} %get-tuple-element.25.wk_ref, f32[16,1024]{1,0:T(8,128)} %get-tuple-element.26.wv_ref, bf16[16,8,640]{2,1,0:T(8,128)(2,1)} %get-tuple-element.27.rows_ref), custom_call_target="tpu_custom_call" | custom-call | tf_op jit(solution)/shard_map/pallas_call | solution.py:434

commit v4 on v3

--- a/solution.py
+++ b/solution.py
@@ -29,8 +29,18 @@
     )
 
 
-def relay(d):
-    return 3 * ((d - 1) // 3)
+GATHER_SPAN = 2
+REDUCE_SPAN = 2
+
+
+def relay(d, span):
+    return span * ((d - 1) // span)
+
+
+def reach(me, span):
+    chips = sorted({1, span} | set(range(1, span + 1)))
+    steps = [1] + [2 * c for c in chips]
+    return [{"ctx": lax.rem(me + d, 32)} for d in steps + [32 - d for d in steps]]
 
 
 def gather_kernel(
@@ -44,6 +54,7 @@
     partner = me + 1 - 2 * core
     mate = {"ctx": partner}
     counts = (7, 8)
+    span = GATHER_SPAN
     width = uk_ref.shape[1]
 
     item[:, :width] = uk_ref[...]
@@ -66,14 +77,14 @@
         return lax.rem(base + n - 2 * d, n) if way == 0 else lax.rem(base + 2 * d, n)
 
     def send(way, d):
-        slot = buf.at[origin(me, way, relay(d))]
-        src = item if relay(d) == 0 else slot
-        peer = {"ctx": away(way, d - relay(d))}
+        slot = buf.at[origin(me, way, relay(d, span))]
+        src = item if relay(d, span) == 0 else slot
+        peer = {"ctx": away(way, d - relay(d, span))}
         return remote(src, slot, ring_send.at[way, d], ring_recv.at[way, d], peer)
 
     def arrival(way, d):
         slot = buf.at[origin(me, way, d)]
-        peer = {"ctx": away(1 - way, d - relay(d))}
+        peer = {"ctx": away(1 - way, d - relay(d, span))}
         return remote(slot, slot, ring_send.at[way, d], ring_recv.at[way, d], peer)
 
     def mate_copy(way, d, base):
@@ -85,8 +96,8 @@
     halo_mate = remote(win.at[2 - 2 * core], win.at[1], halo_send.at[1], halo_recv.at[1], mate)
     ways = (1, 0)
 
-    greet([{"ctx": lax.rem(me + d, n)} for d in (1, 2, 4, 6, n - 1, n - 2, n - 4, n - 6)])
-    for d in (3, 2, 1):
+    greet(reach(me, span))
+    for d in range(span, 0, -1):
         for way in ways:
             send(way, d).start()
     own = [
@@ -97,36 +108,22 @@
         copy.start()
     mate_copy(0, 0, me).start()
     halo.start()
-    for way in ways:
-        arrival(way, 3).wait_recv()
-        for d in (6, 5, 4):
-            send(way, d).start()
-    for d in (1, 2):
-        for way in ways:
-            arrival(way, d).wait_recv()
-    for d in (1, 2, 3):
-        for way in ways:
-            mate_copy(way, d, me).start()
-    for way in ways:
-        arrival(way, 6).wait_recv()
-        for d in (8, 7):
-            if d <= counts[way]:
-                send(way, d).start()
+    for top in range(span, 8 + span, span):
+        if top < 8:
+            for way in ways:
+                arrival(way, top).wait_recv()
+                for d in range(min(top + span, counts[way]), top, -1):
+                    send(way, d).start()
+        for d in range(top - span + 1, min(top, 8) + 1):
+            for way in ways:
+                if d <= counts[way]:
+                    if d < top or top >= 8:
+                        arrival(way, d).wait_recv()
+                    mate_copy(way, d, me).start()
     for copy in own:
         copy.wait()
     halo.wait_recv()
     halo_mate.start()
-    for d in (4, 5):
-        for way in ways:
-            arrival(way, d).wait_recv()
-    for d in (4, 5, 6):
-        for way in ways:
-            mate_copy(way, d, me).start()
-    for d in (7, 8):
-        for way in ways:
-            if d <= counts[way]:
-                arrival(way, d).wait_recv()
-                mate_copy(way, d, me).start()
     mate_copy(0, 0, me).wait_send()
     mate_copy(0, 0, partner).wait_recv()
     for d in range(1, 9):
@@ -290,6 +287,7 @@
     partner = me + 1 - 2 * core
     mate = {"ctx": partner}
     counts = (8, 7)
+    span = REDUCE_SPAN
     others = [lax.rem(col + k, m) for k in range(1, m)]
     width = ok.shape[1]
 
@@ -314,7 +312,7 @@
         return remote(mine, final.at[k], all_send.at[k - 1], all_recv.at[k - 1], {"dp": others[k - 1]})
 
     def ring(way, d):
-        peer = {"ctx": away(way, d - relay(d))}
+        peer = {"ctx": away(way, d - relay(d, span))}
         return remote(
             send_buf.at[way, d], recv_buf.at[way, d], ring_send.at[way, d], ring_recv.at[way, d], peer
         )
@@ -332,14 +330,13 @@
 
     def pass_on(way, d):
         total = local(d if way == 0 else 16 - d)
-        if d in (3, 6):
-            total = total + arrived(way, d + 1, d + 3)
+        if d % span == 0 and d < 8:
+            total = total + arrived(way, d + 1, d + span)
         send_buf[way, d] = total.astype(bf16)
         ring(way, d).start()
 
     greet(
-        [{"ctx": lax.rem(me + d, n)} for d in (1, 2, 4, 6, n - 1, n - 2, n - 4, n - 6)]
-        + [{"dp": k} for k in others]
+        reach(me, span) + [{"dp": k} for k in others]
     )
     order = (8, 7, 9, 5, 11, 4, 12, 2, 14, 1, 15, 6, 10, 3, 13, 0)
     for d in order[:3]:
@@ -348,12 +345,11 @@
         mix_copy(k).start()
     for d in order[3:]:
         to_mate(d).start()
-    for d in (8, 7, 5, 4):
+    plan = {1: (8, 7, 6, 5, 4, 3, 2, 1), 2: (8, 7, 5, 6, 3, 4, 1, 2), 3: (8, 7, 5, 4, 6, 2, 1, 3)}[span]
+    for d in plan[:4]:
         for way in range(2):
             if d <= counts[way]:
                 pass_on(way, d)
-    for way in range(2):
-        pass_on(way, 6)
     total = dl[col].astype(f32)
     for k in range(1, m):
         mix_copy(k).wait_recv()
@@ -362,7 +358,7 @@
     halves[1] = total[0].astype(bf16)
     for d in (2, 1):
         back_copy(d).start()
-    for d in (2, 1, 3):
+    for d in plan[4:]:
         for way in range(2):
             pass_on(way, d)
     total = total[2]
@@ -376,7 +372,7 @@
     final[0] = rows
     for k in range(1, m):
         all_copy(k).start()
-    total = local(0) + arrived(0, 1, 3) + arrived(1, 1, 3)
+    total = local(0) + arrived(0, 1, span) + arrived(1, 1, span)
     ok[...] = total[:, :width]
     ov[...] = total[:, width:]
     for k in range(1, m):

time: 91.2 us -> 85.1 us (0.933); the launches traced: 90.9 us -> 83.6 us
  Pallas kernels: 89.6 us -> 82.3 us
    pallas_call x1, Pallas kernels: 34 us -> 29.3 us  [reduce(): pl.pallas_call(reduce_kernel, out_shape=(jax.ShapeDtypeStruct((16, width)...]
    pallas_call x1, Pallas kernels: 41.8 us -> 39.2 us  [gather(): pl.pallas_call(gather_kernel, out_shape=(jax.ShapeDtypeStruct((32, 16, to...]
where the time goes in v4:
time: 85.1 us; the launch traced here: 83.6 us
  Pallas kernels  82.3 us (97%)
  between operations  1.3 us (2%)
    pallas_call x1, Pallas kernels, gather(): pl.pallas_call(gather_kernel, out_shape=(jax.ShapeDtypeStruct((32, 16, to...  39.2 us
    pallas_call x1, Pallas kernels, reduce(): pl.pallas_call(reduce_kernel, out_shape=(jax.ShapeDtypeStruct((16, width)...  29.3 us
    pallas_call x1, Pallas kernels, attend(): pl.pallas_call(attend_kernel, grid=(width // 256,), out_shape=(jax.ShapeD...  12.1 us
    pallas_call x1, Pallas kernels, place(): pl.pallas_call(place_kernel, out_shape=(jax.ShapeDtypeStruct(wk.shape, f3...  1.73 us

profile of v4, /device:TPU:1, one launch (start us, length us, event | category | flops | bytes accessed | tf_op | source)
XLA Modules:
  0.0 83.6 jit_solution(6358120838920835658)
XLA Ops:
  1.3 39.2 %shard_map.154 = (bf16[32,16,2176]{2,1,0:T(8,128)(2,1)}, bf16[3,128,640]{2,1,0:T(8,128)(2,1)}) custom-call(bf16[16,1024]{1,0:T(8,128)(2,1)} %uk_ref.1, bf16[16,1024]{1,0:T(8,128)(2,1)} %uv_ref.1, bf16[128,512]{1,0:T(8,128)(2,1)} %lat_ref.1, bf16[64,128]{1,0:T(8,128)(2,1)} %bitcast.15, f32[1,128]{1,0:T(1,128)} %bitcast.16, s32[1,128]{1,0:T(1,128)} %bitcast.17, ...), custom_call_target="tpu_custom_call" | custom-call | tf_op jit(solution)/shard_map/pallas_call | solution.py:143
  40.5 12.1 %shard_map.155 = (bf16[128,1024]{1,0:T(8,128)(2,1)}, bf16[128,512]{1,0:T(8,128)(2,1)}, bf16[512,2048]{1,0:T(8,128)(2,1)}, bf16[16,3,8,640]{3,2,1,0:T(8,128)(2,1)}) custom-call(bf16[384,640]{1,0:T(8,128)(2,1)} %bitcast.14, bf16[512,2176]{1,0:T(8,128)(2,1)} %bitcast.10, bf16[512,2176]{1,0:T(8,128)(2,1)} %bitcast.11, bf16[128,1024]{1,0:T(8,128)(2,1)} %q_ref.1, ...), custom_call_target="tpu_custom_call" | custom-call | tf_op jit(solution)/shard_map/pallas_call | solution.py:257
  52.5 29.3 %shard_map.156 = (f32[16,1024]{1,0:T(8,128)}, f32[16,1024]{1,0:T(8,128)}, bf16[16,8,640]{2,1,0:T(8,128)(2,1)}) custom-call(bf16[32,16,2048]{2,1,0:T(8,128)(2,1)} %bitcast.13, bf16[16,3,8,640]{3,2,1,0:T(8,128)(2,1)} %get-tuple-element.24.dl), custom_call_target="tpu_custom_call" | custom-call | tf_op jit(solution)/shard_map/pallas_call | solution.py:395
  81.9 1.7 %shard_map.157 = (f32[16,1024]{1,0:T(8,128)}, f32[16,1024]{1,0:T(8,128)}, bf16[128,512]{1,0:T(8,128)(2,1)}, bf16[64,128]{1,0:T(8,128)(2,1)}) custom-call(f32[16,1024]{1,0:T(8,128)} %get-tuple-element.25.wk_ref, f32[16,1024]{1,0:T(8,128)} %get-tuple-element.26.wv_ref, bf16[16,8,640]{2,1,0:T(8,128)(2,1)} %get-tuple-element.27.rows_ref), custom_call_target="tpu_custom_call" | custom-call | tf_op jit(solution)/shard_map/pallas_call | solution.py:430

commit v5 on v4

--- a/solution.py
+++ b/solution.py
@@ -16,11 +16,19 @@
 bf16 = jnp.bfloat16
 
 
-def greet(peers):
+def announce(peers):
     barrier = pltpu.get_barrier_semaphore()
     for peer in peers:
         pl.semaphore_signal(barrier, inc=1, device_id=peer, device_id_type=MESH)
-    pl.semaphore_wait(barrier, len(peers))
+
+
+def await_peers(peers):
+    pl.semaphore_wait(pltpu.get_barrier_semaphore(), len(peers))
+
+
+def greet(peers):
+    announce(peers)
+    await_peers(peers)
 
 
 def remote(src, dst, send, recv, peer):
@@ -57,6 +65,8 @@
     span = GATHER_SPAN
     width = uk_ref.shape[1]
 
+    peers = reach(me, span)
+    announce(peers)
     item[:, :width] = uk_ref[...]
     item[:, width:2 * width] = uv_ref[...]
     mask = mask_ref[...].astype(f32)
@@ -96,7 +106,7 @@
     halo_mate = remote(win.at[2 - 2 * core], win.at[1], halo_send.at[1], halo_recv.at[1], mate)
     ways = (1, 0)
 
-    greet(reach(me, span))
+    await_peers(peers)
     for d in range(span, 0, -1):
         for way in ways:
             send(way, d).start()
@@ -338,7 +348,7 @@
     greet(
         reach(me, span) + [{"dp": k} for k in others]
     )
-    order = (8, 7, 9, 5, 11, 4, 12, 2, 14, 1, 15, 6, 10, 3, 13, 0)
+    order = (8, 7, 9, 5, 11, 6, 10, 3, 13, 4, 12, 1, 15, 2, 14, 0)
     for d in order[:3]:
         to_mate(d).start()
     for k in range(1, m):
@@ -358,7 +368,7 @@
     halves[1] = total[0].astype(bf16)
     for d in (2, 1):
         back_copy(d).start()
-    for d in plan[4:]:
+    for d in plan[4:6]:
         for way in range(2):
             pass_on(way, d)
     total = total[2]
@@ -372,6 +382,9 @@
     final[0] = rows
     for k in range(1, m):
         all_copy(k).start()
+    for d in plan[6:]:
+        for way in range(2):
+            pass_on(way, d)
     total = local(0) + arrived(0, 1, span) + arrived(1, 1, span)
     ok[...] = total[:, :width]
     ov[...] = total[:, width:]

time: 85.1 us -> 85.8 us (level)
  the two profiles are of different devices: /device:TPU:1 before, /device:TPU:32 now
where the time goes in v5:
time: 85.8 us; the launch traced here: 85.6 us
  Pallas kernels  84.3 us (98%)
  between operations  1.3 us (2%)
    pallas_call x1, Pallas kernels, gather(): pl.pallas_call(gather_kernel, out_shape=(jax.ShapeDtypeStruct((32, 16, to...  35.9 us
    pallas_call x1, Pallas kernels, reduce(): pl.pallas_call(reduce_kernel, out_shape=(jax.ShapeDtypeStruct((16, width)...  34.6 us
    pallas_call x1, Pallas kernels, attend(): pl.pallas_call(attend_kernel, grid=(width // 256,), out_shape=(jax.ShapeD...  12.1 us
    pallas_call x1, Pallas kernels, place(): pl.pallas_call(place_kernel, out_shape=(jax.ShapeDtypeStruct(wk.shape, f3...  1.73 us

profile of v5, /device:TPU:32, one launch (start us, length us, event | category | flops | bytes accessed | tf_op | source)
XLA Modules:
  0.0 85.6 jit_solution(15435942095329055274)
XLA Ops:
  1.3 35.9 %shard_map.154 = (bf16[32,16,2176]{2,1,0:T(8,128)(2,1)}, bf16[3,128,640]{2,1,0:T(8,128)(2,1)}) custom-call(bf16[16,1024]{1,0:T(8,128)(2,1)} %uk_ref.1, bf16[16,1024]{1,0:T(8,128)(2,1)} %uv_ref.1, bf16[128,512]{1,0:T(8,128)(2,1)} %lat_ref.1, bf16[64,128]{1,0:T(8,128)(2,1)} %bitcast.15, f32[1,128]{1,0:T(1,128)} %bitcast.16, s32[1,128]{1,0:T(1,128)} %bitcast.17, ...), custom_call_target="tpu_custom_call" | custom-call | tf_op jit(solution)/shard_map/pallas_call | solution.py:153
  37.2 12.1 %shard_map.155 = (bf16[128,1024]{1,0:T(8,128)(2,1)}, bf16[128,512]{1,0:T(8,128)(2,1)}, bf16[512,2048]{1,0:T(8,128)(2,1)}, bf16[16,3,8,640]{3,2,1,0:T(8,128)(2,1)}) custom-call(bf16[384,640]{1,0:T(8,128)(2,1)} %bitcast.14, bf16[512,2176]{1,0:T(8,128)(2,1)} %bitcast.10, bf16[512,2176]{1,0:T(8,128)(2,1)} %bitcast.11, bf16[128,1024]{1,0:T(8,128)(2,1)} %q_ref.1, ...), custom_call_target="tpu_custom_call" | custom-call | tf_op jit(solution)/shard_map/pallas_call | solution.py:267
  49.3 34.6 %shard_map.156 = (f32[16,1024]{1,0:T(8,128)}, f32[16,1024]{1,0:T(8,128)}, bf16[16,8,640]{2,1,0:T(8,128)(2,1)}) custom-call(bf16[32,16,2048]{2,1,0:T(8,128)(2,1)} %bitcast.13, bf16[16,3,8,640]{3,2,1,0:T(8,128)(2,1)} %get-tuple-element.24.dl), custom_call_target="tpu_custom_call" | custom-call | tf_op jit(solution)/shard_map/pallas_call | solution.py:408
  83.8 1.7 %shard_map.157 = (f32[16,1024]{1,0:T(8,128)}, f32[16,1024]{1,0:T(8,128)}, bf16[128,512]{1,0:T(8,128)(2,1)}, bf16[64,128]{1,0:T(8,128)(2,1)}) custom-call(f32[16,1024]{1,0:T(8,128)} %get-tuple-element.25.wk_ref, f32[16,1024]{1,0:T(8,128)} %get-tuple-element.26.wv_ref, bf16[16,8,640]{2,1,0:T(8,128)(2,1)} %get-tuple-element.27.rows_ref), custom_call_target="tpu_custom_call" | custom-call | tf_op jit(solution)/shard_map/pallas_call | solution.py:443
